TPU v7x, 128 devices: a whole 4x4x4 slice. The times are simulated.
128 devices in a mesh: blk: 16 (over z, x_hi, core), narrow: 8 (over x_lo, y).
Axes of the slice: x: 4 (x_hi: 2, x_lo: 2; x = x_hi * 2 + x_lo), y: 4, z: 4, core: 2. Of those that a mesh axis runs over, the one named last changes fastest.
Arguments:
- student_img: bfloat16 [16384, 1152], P(('blk', 'narrow')), may hold values from -6 to 6
- student_txt: bfloat16 [16384, 1152], P(('blk', 'narrow')), may hold values from -6 to 6
- teacher_img: bfloat16 [16384, 1536], P(('blk', 'narrow')), may hold values from -6 to 6
- teacher_txt: bfloat16 [16384, 1536], P(('blk', 'narrow')), may hold values from -6 to 6
Outputs:
- image_grad: float32 [16384, 1152], P(('blk', 'narrow'))
- text_grad: float32 [16384, 1152], P(('blk', 'narrow'))
All inputs are finite; a program needn't handle non-finite values.
Results may differ from a plain program's by a relative error of at most 0.0097.
Values may be sent and summed in bfloat16 or wider, within the bound.
A program may use at most 128 MiB of HBM per device.

v0:
```python
import jax
import jax.numpy as jnp
from jax import lax
from jax.sharding import PartitionSpec as P

epsilon = 1e-06
logit_scale = 100.0
logit_bias = -4.0


def shifted(x, axis, by):
    count = lax.axis_size(axis)
    return lax.ppermute(x, axis, [(i, (i + by) % count) for i in range(count)])


def unit_rows(raw_rows):
    raw_float = raw_rows.astype(jnp.float32)
    radius = jnp.sqrt(jnp.sum(raw_float * raw_float, axis=1, keepdims=True) + epsilon)
    return (raw_float / radius, radius)


def unit_back(grad_unit, unit_float, radius):
    along_unit = jnp.sum(unit_float * grad_unit, axis=1, keepdims=True)
    return (grad_unit - unit_float * along_unit) / radius


def body(student_img, student_txt, teacher_img, teacher_txt):
    block_count = lax.axis_size("blk")
    block_index = lax.axis_index("blk")
    group_index = lax.axis_index("narrow")
    own_rows = student_txt.shape[0]
    embed_width = student_txt.shape[1]
    image_block, teacher_block = (
        lax.all_gather(student_img, "narrow", axis=0, tiled=True),
        lax.all_gather(teacher_img, "narrow", axis=0, tiled=True),
    )
    block_rows = image_block.shape[0]
    img_float, img_radius = unit_rows(image_block)
    img_unit = img_float.astype(jnp.bfloat16)
    t_img_unit = unit_rows(teacher_block)[0].astype(jnp.bfloat16)
    txt_float, txt_radius = unit_rows(student_txt)
    txt_unit = txt_float.astype(jnp.bfloat16)
    t_txt_unit = unit_rows(teacher_txt)[0].astype(jnp.bfloat16)
    teacher_tile = (
        logit_scale
        * jnp.einsum(
            "rd,cd->rc",
            t_img_unit,
            lax.all_gather(t_txt_unit, "blk", axis=0, tiled=True),
            preferred_element_type=jnp.float32,
        )
        + logit_bias
    )
    row_ids = lax.broadcasted_iota(jnp.int32, (block_rows, own_rows), 0)
    col_ids = lax.broadcasted_iota(jnp.int32, (block_rows, own_rows), 1) + group_index * own_rows
    same_slot = row_ids == col_ids
    pair_start = jnp.zeros((1, 1), jnp.bfloat16)

    def advance(cycle_step, cycle_state):
        text_cur, teach_cur, grad_acc, img_acc, pair_store = cycle_state
        source = (block_index - cycle_step) % block_count
        teacher_logit = lax.dynamic_slice_in_dim(teacher_tile, source * own_rows, own_rows, 1)
        student_logit = (
            logit_scale
            * jnp.einsum("rd,cd->rc", img_unit, text_cur, preferred_element_type=jnp.float32)
            + logit_bias
        )
        positive = jnp.where(same_slot & (source == block_index), 1.0, 0.0).astype(jnp.float32)
        pair_grad = (
            2.0 * jax.nn.sigmoid(student_logit) - jax.nn.sigmoid(teacher_logit) - positive
        ).astype(jnp.bfloat16)
        img_acc = img_acc + jnp.dot(pair_grad, text_cur, preferred_element_type=jnp.float32)
        grad_acc = grad_acc + jnp.einsum(
            "rc,rd->cd", pair_grad, img_unit, preferred_element_type=jnp.float32
        )
        grad_acc = shifted(grad_acc, "blk", 1)
        text_cur = shifted(text_cur, "blk", 1)
        return (text_cur, teach_cur, grad_acc, img_acc, pair_store)

    start_state = (
        txt_unit,
        t_txt_unit,
        jnp.zeros((own_rows, embed_width), jnp.float32),
        jnp.zeros((block_rows, embed_width), jnp.float32),
        pair_start,
    )
    final_state = lax.fori_loop(0, block_count, advance, start_state)
    grad_acc = final_state[2]
    img_acc = final_state[3]
    pair_store = final_state[4]
    img_grad_unit = lax.psum_scatter(
        logit_scale * img_acc, "narrow", scatter_dimension=0, tiled=True
    )
    own_float = lax.dynamic_slice_in_dim(img_float, group_index * own_rows, own_rows, 0)
    own_radius = lax.dynamic_slice_in_dim(img_radius, group_index * own_rows, own_rows, 0)
    image_grad = unit_back(img_grad_unit, own_float, own_radius)
    txt_grad_unit = logit_scale * grad_acc
    text_grad = unit_back(txt_grad_unit, txt_float, txt_radius)
    return (image_grad, text_grad)


def solution(mesh):
    in_specs = (
        P(("blk", "narrow"), None),
        P(("blk", "narrow"), None),
        P(("blk", "narrow"), None),
        P(("blk", "narrow"), None),
    )
    out_specs = (P(("blk", "narrow"), None), P(("blk", "narrow"), None))
    return jax.shard_map(body, mesh=mesh, in_specs=in_specs, out_specs=out_specs, check_vma=False)
```

profile of v0, /device:TPU:0, one launch (start us, length us, event | category | flops | bytes accessed | tf_op | source)
XLA Modules:
  0.0 578.3 jit_solution(6494705080978374956)
XLA Ops:
  14.8 38.8 %all-gather.4.cloned.1.call-done = bf16[1024,1152]{1,0:T(8,128)(2,1)} async-done(((bf16[128,1152]{1,0:T(8,128)(2,1)}), bf16[1024,1152]{1,0:T(8,128)(2,1)}) %all-gather.4.cloned.1.call-update) | async-done | bytes 2359312 | tf_op jit(solution)/shard_map/all_gather | solution.py:34
  60.3 38.2 %all-gather.6.cloned.1.call-done = bf16[1024,1536]{1,0:T(8,128)(2,1)} async-done(((bf16[128,1536]{1,0:T(8,128)(2,1)}), bf16[1024,1536]{1,0:T(8,128)(2,1)}) %all-gather.6.cloned.1.call-update) | async-done | bytes 3145744 | tf_op jit(solution)/shard_map/all_gather | solution.py:35
  101.1 64.1 %all-gather.8.cloned.1.call-done = bf16[2048,1536]{1,0:T(8,128)(2,1)} async-done(((bf16[128,1536]{1,0:T(8,128)(2,1)}), bf16[2048,1536]{1,0:T(8,128)(2,1)}) %all-gather.8.cloned.1.call-update) | async-done | bytes 6291472 | tf_op jit(solution)/shard_map/all_gather | solution.py:49
  165.2 11.7 %multiply_add_fusion = f32[1024,2048]{1,0:T(8,128)} fusion(bf16[2048,1536]{1,0:T(8,128)(2,1)} %all-gather.8.cloned.1.call-done, bf16[1024,1536]{1,0:T(8,128)(2,1)} %all-gather.6.cloned.1.call-done, f32[1024]{0:T(1024)S(1)} %add_sqrt_fusion), kind=kOutput, calls=%fused_computation.15 | convolution fusion | flops 6451363840 | bytes 17829888 | tf_op jit(solution)/shard_map/rd,cd->rc/dot_general | solution.py:46
  177.0 331.9 %while.20 = (s32[]{:T(128)}, bf16[128,1152]{1,0:T(8,128)(2,1)}, f32[128,1152]{1,0:T(8,128)S(1)}, f32[1024,1152]{1,0:T(8,128)}, bf16[1024,1152]{1,0:T(8,128)(2,1)...) while((s32[]{:T(128)}, bf16[128,1152]{1,0:T(8,128)(2,1)}, ...), condition=%wide.region_5.6_spmd.clone, body=%wide.region_4.5_spmd.clone.sunk | while | flops 910442496 | bytes 21365652 | solution.py:87
  185.0 12.8 %collective-permute-done = bf16[128,1152]{1,0:T(8,128)(2,1)} collective-permute-done((bf16[128,1152]{1,0:T(8,128)(2,1)S(1)}, bf16[128,1152]{1,0:T(8,128)(2,1)}, u32[]{:S(2)}, u32[]{:S(2)}) %collective-permute-start) | collective-permute-done | bytes 294944 | tf_op jit(solution)/shard_map/while/body/eval_jaxpr/ppermute | solution.py:13
  202.1 5.3 convolution_add_fusion.5
  207.4 11.1 %collective-permute-done = bf16[128,1152]{1,0:T(8,128)(2,1)} collective-permute-done((bf16[128,1152]{1,0:T(8,128)(2,1)S(1)}, bf16[128,1152]{1,0:T(8,128)(2,1)}, u32[]{:S(2)}, u32[]{:S(2)}) %collective-permute-start) | collective-permute-done | bytes 294944 | tf_op jit(solution)/shard_map/while/body/eval_jaxpr/ppermute | solution.py:13
  222.9 5.3 convolution_add_fusion.5
  228.2 11.1 %collective-permute-done = bf16[128,1152]{1,0:T(8,128)(2,1)} collective-permute-done((bf16[128,1152]{1,0:T(8,128)(2,1)S(1)}, bf16[128,1152]{1,0:T(8,128)(2,1)}, u32[]{:S(2)}, u32[]{:S(2)}) %collective-permute-start) | collective-permute-done | bytes 294944 | tf_op jit(solution)/shard_map/while/body/eval_jaxpr/ppermute | solution.py:13
  243.6 5.3 convolution_add_fusion.5
  248.9 11.1 %collective-permute-done = bf16[128,1152]{1,0:T(8,128)(2,1)} collective-permute-done((bf16[128,1152]{1,0:T(8,128)(2,1)S(1)}, bf16[128,1152]{1,0:T(8,128)(2,1)}, u32[]{:S(2)}, u32[]{:S(2)}) %collective-permute-start) | collective-permute-done | bytes 294944 | tf_op jit(solution)/shard_map/while/body/eval_jaxpr/ppermute | solution.py:13
  269.6 11.1 %collective-permute-done = bf16[128,1152]{1,0:T(8,128)(2,1)} collective-permute-done((bf16[128,1152]{1,0:T(8,128)(2,1)S(1)}, bf16[128,1152]{1,0:T(8,128)(2,1)}, u32[]{:S(2)}, u32[]{:S(2)}) %collective-permute-start) | collective-permute-done | bytes 294944 | tf_op jit(solution)/shard_map/while/body/eval_jaxpr/ppermute | solution.py:13
  285.1 5.3 convolution_add_fusion.5
  290.4 11.1 %collective-permute-done = bf16[128,1152]{1,0:T(8,128)(2,1)} collective-permute-done((bf16[128,1152]{1,0:T(8,128)(2,1)S(1)}, bf16[128,1152]{1,0:T(8,128)(2,1)}, u32[]{:S(2)}, u32[]{:S(2)}) %collective-permute-start) | collective-permute-done | bytes 294944 | tf_op jit(solution)/shard_map/while/body/eval_jaxpr/ppermute | solution.py:13
  305.8 5.3 convolution_add_fusion.5
  311.1 11.1 %collective-permute-done = bf16[128,1152]{1,0:T(8,128)(2,1)} collective-permute-done((bf16[128,1152]{1,0:T(8,128)(2,1)S(1)}, bf16[128,1152]{1,0:T(8,128)(2,1)}, u32[]{:S(2)}, u32[]{:S(2)}) %collective-permute-start) | collective-permute-done | bytes 294944 | tf_op jit(solution)/shard_map/while/body/eval_jaxpr/ppermute | solution.py:13
  331.9 11.1 %collective-permute-done = bf16[128,1152]{1,0:T(8,128)(2,1)} collective-permute-done((bf16[128,1152]{1,0:T(8,128)(2,1)S(1)}, bf16[128,1152]{1,0:T(8,128)(2,1)}, u32[]{:S(2)}, u32[]{:S(2)}) %collective-permute-start) | collective-permute-done | bytes 294944 | tf_op jit(solution)/shard_map/while/body/eval_jaxpr/ppermute | solution.py:13
  347.3 5.3 convolution_add_fusion.5
  352.6 11.1 %collective-permute-done = bf16[128,1152]{1,0:T(8,128)(2,1)} collective-permute-done((bf16[128,1152]{1,0:T(8,128)(2,1)S(1)}, bf16[128,1152]{1,0:T(8,128)(2,1)}, u32[]{:S(2)}, u32[]{:S(2)}) %collective-permute-start) | collective-permute-done | bytes 294944 | tf_op jit(solution)/shard_map/while/body/eval_jaxpr/ppermute | solution.py:13
  368.1 5.3 convolution_add_fusion.5
  373.3 11.1 %collective-permute-done = bf16[128,1152]{1,0:T(8,128)(2,1)} collective-permute-done((bf16[128,1152]{1,0:T(8,128)(2,1)S(1)}, bf16[128,1152]{1,0:T(8,128)(2,1)}, u32[]{:S(2)}, u32[]{:S(2)}) %collective-permute-start) | collective-permute-done | bytes 294944 | tf_op jit(solution)/shard_map/while/body/eval_jaxpr/ppermute | solution.py:13
  394.1 11.1 %collective-permute-done = bf16[128,1152]{1,0:T(8,128)(2,1)} collective-permute-done((bf16[128,1152]{1,0:T(8,128)(2,1)S(1)}, bf16[128,1152]{1,0:T(8,128)(2,1)}, u32[]{:S(2)}, u32[]{:S(2)}) %collective-permute-start) | collective-permute-done | bytes 294944 | tf_op jit(solution)/shard_map/while/body/eval_jaxpr/ppermute | solution.py:13
  409.5 5.3 convolution_add_fusion.5
  414.8 11.1 %collective-permute-done = bf16[128,1152]{1,0:T(8,128)(2,1)} collective-permute-done((bf16[128,1152]{1,0:T(8,128)(2,1)S(1)}, bf16[128,1152]{1,0:T(8,128)(2,1)}, u32[]{:S(2)}, u32[]{:S(2)}) %collective-permute-start) | collective-permute-done | bytes 294944 | tf_op jit(solution)/shard_map/while/body/eval_jaxpr/ppermute | solution.py:13
  435.6 11.1 %collective-permute-done = bf16[128,1152]{1,0:T(8,128)(2,1)} collective-permute-done((bf16[128,1152]{1,0:T(8,128)(2,1)S(1)}, bf16[128,1152]{1,0:T(8,128)(2,1)}, u32[]{:S(2)}, u32[]{:S(2)}) %collective-permute-start) | collective-permute-done | bytes 294944 | tf_op jit(solution)/shard_map/while/body/eval_jaxpr/ppermute | solution.py:13
  451.0 5.3 convolution_add_fusion.5
  456.3 11.1 %collective-permute-done = bf16[128,1152]{1,0:T(8,128)(2,1)} collective-permute-done((bf16[128,1152]{1,0:T(8,128)(2,1)S(1)}, bf16[128,1152]{1,0:T(8,128)(2,1)}, u32[]{:S(2)}, u32[]{:S(2)}) %collective-permute-start) | collective-permute-done | bytes 294944 | tf_op jit(solution)/shard_map/while/body/eval_jaxpr/ppermute | solution.py:13
  471.8 5.3 convolution_add_fusion.5
  477.1 11.1 %collective-permute-done = bf16[128,1152]{1,0:T(8,128)(2,1)} collective-permute-done((bf16[128,1152]{1,0:T(8,128)(2,1)S(1)}, bf16[128,1152]{1,0:T(8,128)(2,1)}, u32[]{:S(2)}, u32[]{:S(2)}) %collective-permute-start) | collective-permute-done | bytes 294944 | tf_op jit(solution)/shard_map/while/body/eval_jaxpr/ppermute | solution.py:13
  497.8 11.1 %collective-permute-done = bf16[128,1152]{1,0:T(8,128)(2,1)} collective-permute-done((bf16[128,1152]{1,0:T(8,128)(2,1)S(1)}, bf16[128,1152]{1,0:T(8,128)(2,1)}, u32[]{:S(2)}, u32[]{:S(2)}) %collective-permute-start) | collective-permute-done | bytes 294944 | tf_op jit(solution)/shard_map/while/body/eval_jaxpr/ppermute | solution.py:13
  515.9 52.3 %reduce-scatter.2.cloned.1.call-done = f32[128,1152]{1,0:T(8,128)} async-done(((f32[1024,1152]{1,0:T(8,128)}), f32[128,1152]{1,0:T(8,128)}) %reduce-scatter.2.cloned.1.call-update) | async-done | bytes 589840 | tf_op jit(solution)/shard_map/reduce_scatter | solution.py:91
  (132 shorter events, 127.0 us)
Async XLA Ops:
  7.2 46.4 %all-gather.4.cloned.1.call-start = ((), (), s32[]{:S(2)}) async-start(), calls=%async_computation.1 | async-start | bytes 2654208 | tf_op jit(solution)/shard_map/all_gather | solution.py:34
  7.9 90.6 %all-gather.6.cloned.1.call-start = ((), (), s32[]{:S(2)}) async-start(), calls=%async_computation.2 | async-start | bytes 3538944 | tf_op jit(solution)/shard_map/all_gather | solution.py:35
  8.6 156.6 %all-gather.8.cloned.1.call-start = ((), (), s32[]{:S(2)}) async-start(), calls=%async_computation.3 | async-start | bytes 6684672 | tf_op jit(solution)/shard_map/all_gather | solution.py:49
  11.8 556.4 %reduce-scatter.2.cloned.1.call-start = ((), (), s32[]{:S(2)}) async-start(), calls=%async_computation.4 | async-start | bytes 5308416 | tf_op jit(solution)/shard_map/reduce_scatter | solution.py:91
  181.4 16.4 %collective-permute-start.1 = (f32[128,1152]{1,0:T(8,128)}, f32[128,1152]{1,0:T(8,128)S(1)}, u32[]{:S(2)}, u32[]{:S(2)}) collective-permute-start(f32[128,1152]{1,0:T(8,128)} %convolution_add_fusion.4), channel_id=1, source_target_pairs={{0,8},{8,16},{16,24},{24,32},{32,40},{40,48},{48,56},{56,64},{64,7... | collective-permute-start | bytes 1769480 | tf_op jit(solution)/shard_map/while/body/eval_jaxpr/ppermute | solution.py:13
  202.1 16.4 %collective-permute-start.1 = (f32[128,1152]{1,0:T(8,128)}, f32[128,1152]{1,0:T(8,128)S(1)}, u32[]{:S(2)}, u32[]{:S(2)}) collective-permute-start(f32[128,1152]{1,0:T(8,128)} %convolution_add_fusion.4), channel_id=1, source_target_pairs={{0,8},{8,16},{16,24},{24,32},{32,40},{40,48},{48,56},{56,64},{64,7... | collective-permute-start | bytes 1769480 | tf_op jit(solution)/shard_map/while/body/eval_jaxpr/ppermute | solution.py:13
  202.1 16.4 %collective-permute-start = (bf16[128,1152]{1,0:T(8,128)(2,1)S(1)}, bf16[128,1152]{1,0:T(8,128)(2,1)}, u32[]{:S(2)}, u32[]{:S(2)}) collective-permute-start(bf16[128,1152]{1,0:T(8,128)(2,1)S(1)} %copy.11), channel_id=1, source_target_pairs={{0,8},{8,16},{16,24},{24,32},{32,40},{40,48},{48,56},{56,64},{64,7... | collective-permute-start | bytes 884744 | tf_op jit(solution)/shard_map/while/body/eval_jaxpr/ppermute | solution.py:13
  222.9 16.4 %collective-permute-start.1 = (f32[128,1152]{1,0:T(8,128)}, f32[128,1152]{1,0:T(8,128)S(1)}, u32[]{:S(2)}, u32[]{:S(2)}) collective-permute-start(f32[128,1152]{1,0:T(8,128)} %convolution_add_fusion.4), channel_id=1, source_target_pairs={{0,8},{8,16},{16,24},{24,32},{32,40},{40,48},{48,56},{56,64},{64,7... | collective-permute-start | bytes 1769480 | tf_op jit(solution)/shard_map/while/body/eval_jaxpr/ppermute | solution.py:13
  243.6 16.4 %collective-permute-start.1 = (f32[128,1152]{1,0:T(8,128)}, f32[128,1152]{1,0:T(8,128)S(1)}, u32[]{:S(2)}, u32[]{:S(2)}) collective-permute-start(f32[128,1152]{1,0:T(8,128)} %convolution_add_fusion.4), channel_id=1, source_target_pairs={{0,8},{8,16},{16,24},{24,32},{32,40},{40,48},{48,56},{56,64},{64,7... | collective-permute-start | bytes 1769480 | tf_op jit(solution)/shard_map/while/body/eval_jaxpr/ppermute | solution.py:13
  243.6 16.4 %collective-permute-start = (bf16[128,1152]{1,0:T(8,128)(2,1)S(1)}, bf16[128,1152]{1,0:T(8,128)(2,1)}, u32[]{:S(2)}, u32[]{:S(2)}) collective-permute-start(bf16[128,1152]{1,0:T(8,128)(2,1)S(1)} %copy.11), channel_id=1, source_target_pairs={{0,8},{8,16},{16,24},{24,32},{32,40},{40,48},{48,56},{56,64},{64,7... | collective-permute-start | bytes 884744 | tf_op jit(solution)/shard_map/while/body/eval_jaxpr/ppermute | solution.py:13
  264.4 16.4 %collective-permute-start.1 = (f32[128,1152]{1,0:T(8,128)}, f32[128,1152]{1,0:T(8,128)S(1)}, u32[]{:S(2)}, u32[]{:S(2)}) collective-permute-start(f32[128,1152]{1,0:T(8,128)} %convolution_add_fusion.4), channel_id=1, source_target_pairs={{0,8},{8,16},{16,24},{24,32},{32,40},{40,48},{48,56},{56,64},{64,7... | collective-permute-start | bytes 1769480 | tf_op jit(solution)/shard_map/while/body/eval_jaxpr/ppermute | solution.py:13
  264.4 16.4 %collective-permute-start = (bf16[128,1152]{1,0:T(8,128)(2,1)S(1)}, bf16[128,1152]{1,0:T(8,128)(2,1)}, u32[]{:S(2)}, u32[]{:S(2)}) collective-permute-start(bf16[128,1152]{1,0:T(8,128)(2,1)S(1)} %copy.11), channel_id=1, source_target_pairs={{0,8},{8,16},{16,24},{24,32},{32,40},{40,48},{48,56},{56,64},{64,7... | collective-permute-start | bytes 884744 | tf_op jit(solution)/shard_map/while/body/eval_jaxpr/ppermute | solution.py:13
  285.1 16.4 %collective-permute-start.1 = (f32[128,1152]{1,0:T(8,128)}, f32[128,1152]{1,0:T(8,128)S(1)}, u32[]{:S(2)}, u32[]{:S(2)}) collective-permute-start(f32[128,1152]{1,0:T(8,128)} %convolution_add_fusion.4), channel_id=1, source_target_pairs={{0,8},{8,16},{16,24},{24,32},{32,40},{40,48},{48,56},{56,64},{64,7... | collective-permute-start | bytes 1769480 | tf_op jit(solution)/shard_map/while/body/eval_jaxpr/ppermute | solution.py:13
  305.8 16.4 %collective-permute-start.1 = (f32[128,1152]{1,0:T(8,128)}, f32[128,1152]{1,0:T(8,128)S(1)}, u32[]{:S(2)}, u32[]{:S(2)}) collective-permute-start(f32[128,1152]{1,0:T(8,128)} %convolution_add_fusion.4), channel_id=1, source_target_pairs={{0,8},{8,16},{16,24},{24,32},{32,40},{40,48},{48,56},{56,64},{64,7... | collective-permute-start | bytes 1769480 | tf_op jit(solution)/shard_map/while/body/eval_jaxpr/ppermute | solution.py:13
  305.8 16.4 %collective-permute-start = (bf16[128,1152]{1,0:T(8,128)(2,1)S(1)}, bf16[128,1152]{1,0:T(8,128)(2,1)}, u32[]{:S(2)}, u32[]{:S(2)}) collective-permute-start(bf16[128,1152]{1,0:T(8,128)(2,1)S(1)} %copy.11), channel_id=1, source_target_pairs={{0,8},{8,16},{16,24},{24,32},{32,40},{40,48},{48,56},{56,64},{64,7... | collective-permute-start | bytes 884744 | tf_op jit(solution)/shard_map/while/body/eval_jaxpr/ppermute | solution.py:13
  326.6 16.4 %collective-permute-start.1 = (f32[128,1152]{1,0:T(8,128)}, f32[128,1152]{1,0:T(8,128)S(1)}, u32[]{:S(2)}, u32[]{:S(2)}) collective-permute-start(f32[128,1152]{1,0:T(8,128)} %convolution_add_fusion.4), channel_id=1, source_target_pairs={{0,8},{8,16},{16,24},{24,32},{32,40},{40,48},{48,56},{56,64},{64,7... | collective-permute-start | bytes 1769480 | tf_op jit(solution)/shard_map/while/body/eval_jaxpr/ppermute | solution.py:13
  326.6 16.4 %collective-permute-start = (bf16[128,1152]{1,0:T(8,128)(2,1)S(1)}, bf16[128,1152]{1,0:T(8,128)(2,1)}, u32[]{:S(2)}, u32[]{:S(2)}) collective-permute-start(bf16[128,1152]{1,0:T(8,128)(2,1)S(1)} %copy.11), channel_id=1, source_target_pairs={{0,8},{8,16},{16,24},{24,32},{32,40},{40,48},{48,56},{56,64},{64,7... | collective-permute-start | bytes 884744 | tf_op jit(solution)/shard_map/while/body/eval_jaxpr/ppermute | solution.py:13
  347.3 16.4 %collective-permute-start.1 = (f32[128,1152]{1,0:T(8,128)}, f32[128,1152]{1,0:T(8,128)S(1)}, u32[]{:S(2)}, u32[]{:S(2)}) collective-permute-start(f32[128,1152]{1,0:T(8,128)} %convolution_add_fusion.4), channel_id=1, source_target_pairs={{0,8},{8,16},{16,24},{24,32},{32,40},{40,48},{48,56},{56,64},{64,7... | collective-permute-start | bytes 1769480 | tf_op jit(solution)/shard_map/while/body/eval_jaxpr/ppermute | solution.py:13
  347.3 16.4 %collective-permute-start = (bf16[128,1152]{1,0:T(8,128)(2,1)S(1)}, bf16[128,1152]{1,0:T(8,128)(2,1)}, u32[]{:S(2)}, u32[]{:S(2)}) collective-permute-start(bf16[128,1152]{1,0:T(8,128)(2,1)S(1)} %copy.11), channel_id=1, source_target_pairs={{0,8},{8,16},{16,24},{24,32},{32,40},{40,48},{48,56},{56,64},{64,7... | collective-permute-start | bytes 884744 | tf_op jit(solution)/shard_map/while/body/eval_jaxpr/ppermute | solution.py:13
  368.1 16.4 %collective-permute-start.1 = (f32[128,1152]{1,0:T(8,128)}, f32[128,1152]{1,0:T(8,128)S(1)}, u32[]{:S(2)}, u32[]{:S(2)}) collective-permute-start(f32[128,1152]{1,0:T(8,128)} %convolution_add_fusion.4), channel_id=1, source_target_pairs={{0,8},{8,16},{16,24},{24,32},{32,40},{40,48},{48,56},{56,64},{64,7... | collective-permute-start | bytes 1769480 | tf_op jit(solution)/shard_map/while/body/eval_jaxpr/ppermute | solution.py:13
  368.1 16.4 %collective-permute-start = (bf16[128,1152]{1,0:T(8,128)(2,1)S(1)}, bf16[128,1152]{1,0:T(8,128)(2,1)}, u32[]{:S(2)}, u32[]{:S(2)}) collective-permute-start(bf16[128,1152]{1,0:T(8,128)(2,1)S(1)} %copy.11), channel_id=1, source_target_pairs={{0,8},{8,16},{16,24},{24,32},{32,40},{40,48},{48,56},{56,64},{64,7... | collective-permute-start | bytes 884744 | tf_op jit(solution)/shard_map/while/body/eval_jaxpr/ppermute | solution.py:13
  388.8 16.4 %collective-permute-start.1 = (f32[128,1152]{1,0:T(8,128)}, f32[128,1152]{1,0:T(8,128)S(1)}, u32[]{:S(2)}, u32[]{:S(2)}) collective-permute-start(f32[128,1152]{1,0:T(8,128)} %convolution_add_fusion.4), channel_id=1, source_target_pairs={{0,8},{8,16},{16,24},{24,32},{32,40},{40,48},{48,56},{56,64},{64,7... | collective-permute-start | bytes 1769480 | tf_op jit(solution)/shard_map/while/body/eval_jaxpr/ppermute | solution.py:13
  388.8 16.4 %collective-permute-start = (bf16[128,1152]{1,0:T(8,128)(2,1)S(1)}, bf16[128,1152]{1,0:T(8,128)(2,1)}, u32[]{:S(2)}, u32[]{:S(2)}) collective-permute-start(bf16[128,1152]{1,0:T(8,128)(2,1)S(1)} %copy.11), channel_id=1, source_target_pairs={{0,8},{8,16},{16,24},{24,32},{32,40},{40,48},{48,56},{56,64},{64,7... | collective-permute-start | bytes 884744 | tf_op jit(solution)/shard_map/while/body/eval_jaxpr/ppermute | solution.py:13
  409.5 16.4 %collective-permute-start.1 = (f32[128,1152]{1,0:T(8,128)}, f32[128,1152]{1,0:T(8,128)S(1)}, u32[]{:S(2)}, u32[]{:S(2)}) collective-permute-start(f32[128,1152]{1,0:T(8,128)} %convolution_add_fusion.4), channel_id=1, source_target_pairs={{0,8},{8,16},{16,24},{24,32},{32,40},{40,48},{48,56},{56,64},{64,7... | collective-permute-start | bytes 1769480 | tf_op jit(solution)/shard_map/while/body/eval_jaxpr/ppermute | solution.py:13
  409.5 16.4 %collective-permute-start = (bf16[128,1152]{1,0:T(8,128)(2,1)S(1)}, bf16[128,1152]{1,0:T(8,128)(2,1)}, u32[]{:S(2)}, u32[]{:S(2)}) collective-permute-start(bf16[128,1152]{1,0:T(8,128)(2,1)S(1)} %copy.11), channel_id=1, source_target_pairs={{0,8},{8,16},{16,24},{24,32},{32,40},{40,48},{48,56},{56,64},{64,7... | collective-permute-start | bytes 884744 | tf_op jit(solution)/shard_map/while/body/eval_jaxpr/ppermute | solution.py:13
  430.3 16.4 %collective-permute-start.1 = (f32[128,1152]{1,0:T(8,128)}, f32[128,1152]{1,0:T(8,128)S(1)}, u32[]{:S(2)}, u32[]{:S(2)}) collective-permute-start(f32[128,1152]{1,0:T(8,128)} %convolution_add_fusion.4), channel_id=1, source_target_pairs={{0,8},{8,16},{16,24},{24,32},{32,40},{40,48},{48,56},{56,64},{64,7... | collective-permute-start | bytes 1769480 | tf_op jit(solution)/shard_map/while/body/eval_jaxpr/ppermute | solution.py:13
  430.3 16.4 %collective-permute-start = (bf16[128,1152]{1,0:T(8,128)(2,1)S(1)}, bf16[128,1152]{1,0:T(8,128)(2,1)}, u32[]{:S(2)}, u32[]{:S(2)}) collective-permute-start(bf16[128,1152]{1,0:T(8,128)(2,1)S(1)} %copy.11), channel_id=1, source_target_pairs={{0,8},{8,16},{16,24},{24,32},{32,40},{40,48},{48,56},{56,64},{64,7... | collective-permute-start | bytes 884744 | tf_op jit(solution)/shard_map/while/body/eval_jaxpr/ppermute | solution.py:13
  451.0 16.4 %collective-permute-start.1 = (f32[128,1152]{1,0:T(8,128)}, f32[128,1152]{1,0:T(8,128)S(1)}, u32[]{:S(2)}, u32[]{:S(2)}) collective-permute-start(f32[128,1152]{1,0:T(8,128)} %convolution_add_fusion.4), channel_id=1, source_target_pairs={{0,8},{8,16},{16,24},{24,32},{32,40},{40,48},{48,56},{56,64},{64,7... | collective-permute-start | bytes 1769480 | tf_op jit(solution)/shard_map/while/body/eval_jaxpr/ppermute | solution.py:13
  471.8 16.4 %collective-permute-start.1 = (f32[128,1152]{1,0:T(8,128)}, f32[128,1152]{1,0:T(8,128)S(1)}, u32[]{:S(2)}, u32[]{:S(2)}) collective-permute-start(f32[128,1152]{1,0:T(8,128)} %convolution_add_fusion.4), channel_id=1, source_target_pairs={{0,8},{8,16},{16,24},{24,32},{32,40},{40,48},{48,56},{56,64},{64,7... | collective-permute-start | bytes 1769480 | tf_op jit(solution)/shard_map/while/body/eval_jaxpr/ppermute | solution.py:13
  471.8 16.4 %collective-permute-start = (bf16[128,1152]{1,0:T(8,128)(2,1)S(1)}, bf16[128,1152]{1,0:T(8,128)(2,1)}, u32[]{:S(2)}, u32[]{:S(2)}) collective-permute-start(bf16[128,1152]{1,0:T(8,128)(2,1)S(1)} %copy.11), channel_id=1, source_target_pairs={{0,8},{8,16},{16,24},{24,32},{32,40},{40,48},{48,56},{56,64},{64,7... | collective-permute-start | bytes 884744 | tf_op jit(solution)/shard_map/while/body/eval_jaxpr/ppermute | solution.py:13
  492.5 16.4 %collective-permute-start.1 = (f32[128,1152]{1,0:T(8,128)}, f32[128,1152]{1,0:T(8,128)S(1)}, u32[]{:S(2)}, u32[]{:S(2)}) collective-permute-start(f32[128,1152]{1,0:T(8,128)} %convolution_add_fusion.4), channel_id=1, source_target_pairs={{0,8},{8,16},{16,24},{24,32},{32,40},{40,48},{48,56},{56,64},{64,7... | collective-permute-start | bytes 1769480 | tf_op jit(solution)/shard_map/while/body/eval_jaxpr/ppermute | solution.py:13
  492.5 16.4 %collective-permute-start = (bf16[128,1152]{1,0:T(8,128)(2,1)S(1)}, bf16[128,1152]{1,0:T(8,128)(2,1)}, u32[]{:S(2)}, u32[]{:S(2)}) collective-permute-start(bf16[128,1152]{1,0:T(8,128)(2,1)S(1)} %copy.11), channel_id=1, source_target_pairs={{0,8},{8,16},{16,24},{24,32},{32,40},{40,48},{48,56},{56,64},{64,7... | collective-permute-start | bytes 884744 | tf_op jit(solution)/shard_map/while/body/eval_jaxpr/ppermute | solution.py:13
  (5 other events, 66.3 us)
Sparse Core Ops, SparseCore 0:
  9.6 43.9 all-gather.3
  55.2 43.2 all-gather.5
  101.6 63.6 all-gather.7
  513.8 54.3 reduce-scatter.1
where the time goes:
time: 581 us; the launch traced here: 578 us
  waiting for transfers between devices  374 us (64%)
  matrix products  148 us (25%)
  other arithmetic  24.9 us (4%)
  local copies, waits for them, and re-layouts  16.4 us (3%)
  between operations  13.8 us (2%)
    ppermute x32, waiting for transfers between devices, shifted(): return lax.ppermute(x, axis, [(i, (i + by) % count) for i in range(count)])  179 us
    dot_general x16, matrix products, advance(): jnp.dot(pair_grad, text_cur, preferred_element_type=jnp.float32)  82.2 us
    all_gather x1, waiting for transfers between devices, body(): lax.all_gather(t_txt_unit, 'blk', axis=0, tiled=True)  64.1 us
    reduce_scatter x1, waiting for transfers between devices, body(): lax.psum_scatter(logit_scale * img_acc, 'narrow', scatter_dimension=0, ti...  52.3 us
    all_gather x1, waiting for transfers between devices, body(): lax.all_gather(student_img, 'narrow', axis=0, tiled=True)  38.8 us
    all_gather x1, waiting for transfers between devices, body(): lax.all_gather(teacher_img, 'narrow', axis=0, tiled=True)  38.2 us
    dot_general x16, matrix products, advance(): jnp.einsum('rd,cd->rc', img_unit, text_cur, preferred_element_type=jnp.fl...  32.2 us
    dot_general x16, matrix products, advance(): jnp.einsum('rc,rd->cd', pair_grad, img_unit, preferred_element_type=jnp.f...  21.8 us
  transfers between devices with their start and end apart: 36, of which 20 were waited for; matrix products, arithmetic and copies ran while one was open for 17% of the time, Pallas kernels for 0%

commit v1 on v0

v1 whole, which is shorter than its diff:
```python
import jax
import jax.numpy as jnp
from jax import lax
from jax.experimental import pallas as pl
from jax.experimental.pallas import tpu as pltpu
from jax.sharding import PartitionSpec as P

epsilon = 1e-06
logit_scale = 100.0
logit_bias = -4.0
half_scale = 0.5 * logit_scale
half_bias = 0.5 * logit_bias

ROWS = 128
MESH_ID = pl.DeviceIdType.MESH
NT = (((1,), (1,)), ((), ()))
NN = (((1,), (0,)), ((), ()))
TN = (((0,), (0,)), ((), ()))


def dot(a, b, dims):
    return lax.dot_general(a, b, dims, preferred_element_type=jnp.float32)


def unit_of(raw):
    x = raw.astype(jnp.float32)
    radius = jnp.sqrt(jnp.sum(x * x, axis=1, keepdims=True) + epsilon)
    return x / radius, radius


def back(grad, raw):
    unit, radius = unit_of(raw)
    along = jnp.sum(unit * grad, axis=1, keepdims=True)
    return (grad - unit * along) / radius


def kernel(
    img_raw, txt_raw, timg_raw, ttxt_raw, image_grad, text_grad,
    si, ti, st, tt, gs, iacc, tacc, ib, tb, ts, crecv, irecv, trecv,
    send_si, send_ti, send_st, send_tt, recv_si, recv_ti, recv_st, recv_tt,
    csend_st, csend_tt, crecv_st, crecv_tt, csend_g, crecv_g, isend, irsem, tsend, trsem,
):
    b = lax.axis_index("blk")
    n = lax.axis_index("narrow")
    core = lax.rem(b, 2)
    z = b // 4
    x = 2 * lax.rem(b // 2, 2) + n // 4
    y = lax.rem(n, 4)
    odd = lax.rem(x, 2)

    def device(x, y, z, core):
        return ((z * 2 + x // 2) * 2 + core, lax.rem(x, 2) * 4 + y)

    def step(v, by):
        return lax.rem(v + 4 + by, 4)

    x_img = x + 1 - 2 * odd
    x_txt = lax.rem(x + 3 + 2 * odd, 4)
    img_up = device(x, step(y, 1), z, core)
    img_down = device(x, step(y, -1), z, core)
    img_far = device(x, step(y, 2), z, core)
    img_side = device(x_img, y, z, core)
    txt_up = device(x, y, step(z, 1), core)
    txt_down = device(x, y, step(z, -1), core)
    txt_far = device(x, y, step(z, 2), core)
    txt_side = device(x_txt, y, z, core)
    twin = device(x, y, z, 1 - core)

    barrier = pltpu.get_barrier_semaphore()
    for peer in (img_up, img_down, img_far, img_side, txt_up, txt_down, txt_far, txt_side, twin):
        pl.semaphore_signal(barrier, inc=1, device_id=peer, device_id_type=MESH_ID)

    ti[0:ROWS] = unit_of(timg_raw[...])[0].astype(jnp.bfloat16)
    tt[0:ROWS] = unit_of(ttxt_raw[...])[0].astype(jnp.bfloat16)
    si[0:ROWS] = unit_of(img_raw[...])[0].astype(jnp.bfloat16)
    st[0:ROWS] = unit_of(txt_raw[...])[0].astype(jnp.bfloat16)

    pl.semaphore_wait(barrier, 9)

    sent = []

    def remote(src, dst, ssem, rsem, dev):
        copy = pltpu.make_async_remote_copy(
            src_ref=src, dst_ref=dst, send_sem=ssem, recv_sem=rsem, device_id=dev, device_id_type=MESH_ID
        )
        copy.start()
        sent.append(copy)
        return copy

    arrays = {
        "ti": (ti, send_ti, recv_ti, ROWS, (img_up, img_down, img_side)),
        "si": (si, send_si, recv_si, ROWS, (img_up, img_down, img_side)),
        "tt": (tt, send_tt, recv_tt, 2 * ROWS, (txt_up, txt_down, txt_side)),
        "st": (st, send_st, recv_st, 2 * ROWS, (txt_up, txt_down, txt_side)),
    }
    got = {}

    def hop(name, src, dst, way):
        ref, ssem, rsem, pitch, devs = arrays[name]
        got[name, dst] = remote(
            ref.at[pl.ds(src * pitch, ROWS)], ref.at[pl.ds(dst * pitch, ROWS)],
            ssem.at[dst], rsem.at[dst], devs[way],
        )

    def across(name, place):
        ref, _, _, pitch, _ = arrays[name]
        ssem, rsem = (csend_tt, crecv_tt) if name == "tt" else (csend_st, crecv_st)
        got[name + "c", place] = remote(
            ref.at[pl.ds(place * pitch, ROWS)], ref.at[pl.ds(place * pitch + ROWS, ROWS)],
            ssem.at[place], rsem.at[place], twin,
        )

    def arrive(*keys):
        for key in keys:
            got[key].wait_recv()

    UP, DOWN, SIDE = 0, 1, 2
    for names in (("ti", "tt"), ("si", "st")):
        for name in names:
            hop(name, 0, 2, UP)
            hop(name, 0, 1, DOWN)
            hop(name, 0, 3, SIDE)
    across("tt", 0)
    across("st", 0)

    def clear(i, _):
        rows = pl.ds(pl.multiple_of(i * ROWS, ROWS), ROWS)
        iacc[rows, :] = jnp.zeros((ROWS, iacc.shape[1]), jnp.float32)
        tacc[pl.ds(pl.multiple_of(i * 2 * ROWS, 2 * ROWS), 2 * ROWS), :] = jnp.zeros(
            (2 * ROWS, tacc.shape[1]), jnp.float32
        )
        return 0

    lax.fori_loop(0, 8, clear, 0)

    arrive(("ti", 1), ("tt", 1))
    for name in ("ti", "tt"):
        hop(name, 1, 4, DOWN)
    arrive(("ti", 3), ("tt", 3), ("ti", 2), ("tt", 2))
    for name in ("ti", "tt"):
        hop(name, 3, 6, UP)
        hop(name, 3, 5, DOWN)
    for place in (1, 2, 3):
        across("tt", place)
    arrive(("si", 2), ("st", 2))
    for name in ("si", "st"):
        hop(name, 2, 4, UP)
    arrive(("si", 3), ("st", 3), ("si", 1), ("st", 1))
    for name in ("si", "st"):
        hop(name, 3, 6, UP)
        hop(name, 3, 5, DOWN)
    for place in (1, 2, 3):
        across("st", place)

    def pair_value(zs, zt):
        return 0.5 + jnp.tanh(half_scale * zs + half_bias) - 0.5 * jnp.tanh(half_scale * zt + half_bias)

    def block(first, count, place, diagonal):
        rows = slice(first, first + count)
        cols = pl.ds(pl.multiple_of(place * 2 * ROWS, 2 * ROWS), 2 * ROWS)
        zt = dot(ti[rows], tt[cols, :], NT)
        zs = dot(si[rows], st[cols, :], NT)
        if diagonal:
            row = lax.broadcasted_iota(jnp.int32, (ROWS, 2 * ROWS), 0)
            col = lax.broadcasted_iota(jnp.int32, (ROWS, 2 * ROWS), 1)
            positive = jnp.where(row == col + place * 4 * ROWS, 1.0, 0.0)
            gs[0:ROWS] = (pair_value(zs[:ROWS], zt[:ROWS]) - positive).astype(jnp.bfloat16)
            gs[ROWS:count] = pair_value(zs[ROWS:], zt[ROWS:]).astype(jnp.bfloat16)
        else:
            gs[0:count] = pair_value(zs, zt).astype(jnp.bfloat16)
        g = gs[0:count]
        iacc[rows] += dot(g, st[cols, :], NN)
        tacc[cols, :] += dot(g, si[rows], TN)

    def blocks(first, count, begin, end, diagonal=False):
        def one(place, _):
            block(first, count, place, diagonal)
            return 0

        lax.fori_loop(begin, end, one, 0)

    arrive(*[(name, place) for place in range(4) for name in ("ttc", "stc")])
    blocks(0, 512, 0, 4, True)

    arrive(("ti", 4), ("tt", 4))
    for name in ("ti", "tt"):
        hop(name, 4, 7, SIDE)
    across("tt", 4)
    arrive(("si", 4), ("st", 4))
    for name in ("si", "st"):
        hop(name, 4, 7, SIDE)
    across("st", 4)
    blocks(512, 128, 0, 4)
    arrive(("ttc", 4), ("stc", 4))
    blocks(0, 640, 4, 5)

    for place in (5, 6, 7):
        arrive(("tt", place))
        across("tt", place)
    for place in (5, 6, 7):
        arrive(("st", place))
        across("st", place)
    arrive(*[(name, place) for place in (5, 6, 7) for name in ("ti", "si")])
    blocks(640, 384, 0, 5)

    def give(places):
        for p in places:
            lo = p * 2 * ROWS + ROWS
            tb[p * ROWS : (p + 1) * ROWS] = tacc[lo : lo + ROWS].astype(jnp.bfloat16)
        for p in places:
            rows = pl.ds(p * ROWS, ROWS)
            got["g", p] = remote(tb.at[rows], crecv.at[rows], csend_g.at[p], crecv_g.at[p], twin)

    give(range(5))
    arrive(*[(name, place) for place in (5, 6, 7) for name in ("ttc", "stc")])
    blocks(0, 1024, 5, 8)
    give((5, 6, 7))

    def own_txt(p):
        return tacc[p * 2 * ROWS : p * 2 * ROWS + ROWS] + crecv[p * ROWS : (p + 1) * ROWS].astype(jnp.float32)

    def at(ref, p):
        return ref.at[pl.ds(p * ROWS, ROWS)]

    def put_img(p, slot, dev):
        got["i", slot] = remote(at(ib, p), at(irecv, slot), isend.at[slot], irsem.at[slot], dev)

    def put_txt(p, slot, dev):
        got["t", slot] = remote(at(ts, p), at(trecv, slot), tsend.at[slot], trsem.at[slot], dev)

    def came(ref, slot):
        return ref[slot * ROWS : (slot + 1) * ROWS].astype(jnp.float32)

    for p in (7, 5, 6, 1, 2):
        ib[p * ROWS : (p + 1) * ROWS] = iacc[p * ROWS : (p + 1) * ROWS].astype(jnp.bfloat16)
    put_img(7, 0, img_side)
    put_img(5, 1, img_up)
    put_img(6, 2, img_down)
    put_img(1, 3, img_up)
    put_img(2, 4, img_down)
    arrive(*[("g", p) for p in range(8)])
    for p in (7, 5, 6, 1, 2):
        ts[p * ROWS : (p + 1) * ROWS] = own_txt(p).astype(jnp.bfloat16)
    put_txt(7, 0, txt_side)
    put_txt(5, 1, txt_up)
    put_txt(6, 2, txt_down)
    put_txt(1, 3, txt_up)
    put_txt(2, 4, txt_down)

    arrive(("i", 0))
    ib[4 * ROWS : 5 * ROWS] = (iacc[4 * ROWS : 5 * ROWS] + came(irecv, 0)).astype(jnp.bfloat16)
    put_img(4, 5, img_far)
    arrive(("i", 1), ("i", 2))
    ib[3 * ROWS : 4 * ROWS] = (iacc[3 * ROWS : 4 * ROWS] + came(irecv, 1) + came(irecv, 2)).astype(jnp.bfloat16)
    put_img(3, 6, img_side)
    arrive(("t", 0))
    ts[4 * ROWS : 5 * ROWS] = (own_txt(4) + came(trecv, 0)).astype(jnp.bfloat16)
    put_txt(4, 5, txt_far)
    arrive(("t", 1), ("t", 2))
    ts[3 * ROWS : 4 * ROWS] = (own_txt(3) + came(trecv, 1) + came(trecv, 2)).astype(jnp.bfloat16)
    put_txt(3, 6, txt_side)

    arrive(*[("i", slot) for slot in (3, 4, 5, 6)])
    total = iacc[0:ROWS] + came(irecv, 3) + came(irecv, 4) + came(irecv, 5) + came(irecv, 6)
    image_grad[...] = back(logit_scale * total, img_raw[...])
    arrive(*[("t", slot) for slot in (3, 4, 5, 6)])
    total = own_txt(0) + came(trecv, 3) + came(trecv, 4) + came(trecv, 5) + came(trecv, 6)
    text_grad[...] = back(logit_scale * total, txt_raw[...])

    for copy in sent:
        copy.wait_send()


def body(student_img, student_txt, teacher_img, teacher_txt):
    width = student_img.shape[1]
    t_width = teacher_img.shape[1]
    bf16, f32 = jnp.bfloat16, jnp.float32
    vmem = pl.BlockSpec(memory_space=pltpu.VMEM)
    dma = pltpu.SemaphoreType.DMA((8,))
    return pl.pallas_call(
        kernel,
        out_shape=[jax.ShapeDtypeStruct((ROWS, width), f32)] * 2,
        in_specs=[vmem] * 4,
        out_specs=[vmem] * 2,
        scratch_shapes=[
            pltpu.VMEM((8 * ROWS, width), bf16),
            pltpu.VMEM((8 * ROWS, t_width), bf16),
            pltpu.VMEM((16 * ROWS, width), bf16),
            pltpu.VMEM((16 * ROWS, t_width), bf16),
            pltpu.VMEM((8 * ROWS, 2 * ROWS), bf16),
            pltpu.VMEM((8 * ROWS, width), f32),
            pltpu.VMEM((16 * ROWS, width), f32),
            pltpu.VMEM((8 * ROWS, width), bf16),
            pltpu.VMEM((8 * ROWS, width), bf16),
            pltpu.VMEM((8 * ROWS, width), bf16),
            pltpu.VMEM((8 * ROWS, width), bf16),
            pltpu.VMEM((7 * ROWS, width), bf16),
            pltpu.VMEM((7 * ROWS, width), bf16),
        ]
        + [dma] * 18,
        compiler_params=pltpu.CompilerParams(
            collective_id=0, has_side_effects=True, vmem_limit_bytes=62 << 20
        ),
    )(student_img, student_txt, teacher_img, teacher_txt)


def solution(mesh):
    rows = P(("blk", "narrow"), None)
    return jax.shard_map(body, mesh=mesh, in_specs=(rows,) * 4, out_specs=(rows, rows), check_vma=False)
```

time: 581 us -> 100 us (0.17)
  waiting for transfers between devices: 374 us -> 0 us
  matrix products: 148 us -> 0 us
  Pallas kernels: 0 us -> 96.2 us
  other arithmetic: 24.9 us -> 0 us
  local copies, waits for them, and re-layouts: 16.4 us -> 2.8 us
  between operations: 13.8 us -> 0.65 us
    ppermute x32 -> x0, waiting for transfers between devices: 179 us -> none  [shifted(): return lax.ppermute(x, axis, [(i, (i + by) % count) for i in range(count)])]
    dot_general x49 -> x0, matrix products: 148 us -> none  [the longest x16 82.2 us: advance(): jnp.dot(pair_grad, text_cur, preferred_element_type=jnp.float32)]
    all_gather x3 -> x0, waiting for transfers between devices: 141 us -> none  [the longest x1 64.1 us: body(): lax.all_gather(t_txt_unit, 'blk', axis=0, tiled=True)]
    pallas_call x0 -> x1, Pallas kernels: none -> 96.2 us  [body(): pl.pallas_call(kernel, out_shape=[jax.ShapeDtypeStruct((ROWS, width), f32...]
    reduce_scatter x1 -> x0, waiting for transfers between devices: 52.3 us -> none  [body(): lax.psum_scatter(logit_scale * img_acc, 'narrow', scatter_dimension=0, ti...]
    while x16 -> x0, local copies, waits for them, and re-layouts: 15.4 us -> none
    reduce_sum x6 -> x0, other arithmetic: 8.65 us -> none  [the longest x4 7.02 us: unit_rows(): jnp.sum(raw_float * raw_float, axis=1, keepdims=True) + epsilon]
    div x3 -> x0, other arithmetic: 7.74 us -> none  [the longest x1 4.51 us: unit_rows(): return (raw_float / radius, radius)]
  transfers between devices with their start and end apart: 36 -> 0, of which waited for: 20 -> 0; matrix products, arithmetic and copies ran while one was open for 17% -> 0% of each run, Pallas kernels for 0% -> 0%
where the time goes in v1:
time: 100 us; the launch traced here: 99.6 us
  Pallas kernels  96.2 us (96%)
  local copies, waits for them, and re-layouts  2.8 us (3%)
    pallas_call x1, Pallas kernels, body(): pl.pallas_call(kernel, out_shape=[jax.ShapeDtypeStruct((ROWS, width), f32...  96.2 us
    unnamed x4, local copies, waits for them, and re-layouts  2.8 us

profile of v1, /device:TPU:0, one launch (start us, length us, event | category | flops | bytes accessed | tf_op | source)
XLA Modules:
  0.0 99.6 jit_solution(12637702639748926810)
XLA Ops:
  0.6 96.2 %shard_map.59 = (f32[128,1152]{1,0:T(8,128)}, f32[128,1152]{1,0:T(8,128)}) custom-call(bf16[128,1152]{1,0:T(8,128)(2,1)} %img_raw.1, bf16[128,1152]{1,0:T(8,128)(2,1)} %txt_raw.1, bf16[128,1536]{1,0:T(8,128)(2,1)} %timg_raw.1, bf16[128,1536]{1,0:T(8,128)(2,1)} %ttxt_raw.1), custom_call_target="tpu_custom_call" | custom-call | tf_op jit(solution)/shard_map/pallas_call | solution.py:280
  96.8 0.0 copy-start
  96.8 2.0 %copy.8 = f32[128,1152]{1,0:T(8,128)} copy(f32[128,1152]{1,0:T(8,128)} %get-tuple-element.4) | data formatting | bytes 1179648
  98.8 0.0 copy-done
  98.8 0.8 copy.9
Async XLA Ops:
  96.8 2.0 %copy-start = (f32[128,1152]{1,0:T(8,128)S(1)}, f32[128,1152]{1,0:T(8,128)}, u32[]{:S(2)}) copy-start(f32[128,1152]{1,0:T(8,128)} %get-tuple-element.5) | copy-start | bytes 1769476

commit v2 on v1

v2 whole, which is shorter than its diff:
```python
import jax
import jax.numpy as jnp
from jax import lax
from jax.experimental import pallas as pl
from jax.experimental.pallas import tpu as pltpu
from jax.sharding import PartitionSpec as P

epsilon = 1e-06
logit_scale = 100.0
logit_bias = -4.0
half_scale = 0.5 * logit_scale
half_bias = 0.5 * logit_bias

ROWS = 128
MESH_ID = pl.DeviceIdType.MESH
NT = (((1,), (1,)), ((), ()))
NN = (((1,), (0,)), ((), ()))
TN = (((0,), (0,)), ((), ()))

HALF = ROWS // 2


def dot(a, b, dims):
    return lax.dot_general(a, b, dims, preferred_element_type=jnp.float32)


def unit_of(raw):
    x = raw.astype(jnp.float32)
    radius = jnp.sqrt(jnp.sum(x * x, axis=1, keepdims=True) + epsilon)
    return x / radius, radius


def back(grad, raw):
    unit, radius = unit_of(raw)
    along = jnp.sum(unit * grad, axis=1, keepdims=True)
    return (grad - unit * along) / radius


def kernel(
    img_raw, txt_raw, timg_raw, ttxt_raw, image_grad, text_grad,
    si, ti, st, tt, ps, gs, iacc, tacc, ib, tb, ts, crecv, irecv, trecv,
    send_si, send_ti, send_st, send_tt, recv_si, recv_ti, recv_st, recv_tt,
    csend_st, csend_tt, crecv_st, crecv_tt, csend_g, crecv_g, isend, irsem, tsend, trsem,
):
    b = lax.axis_index("blk")
    n = lax.axis_index("narrow")
    core = lax.rem(b, 2)
    z = b // 4
    x = 2 * lax.rem(b // 2, 2) + n // 4
    y = lax.rem(n, 4)
    odd = lax.rem(x, 2)

    def device(x, y, z, core):
        return ((z * 2 + x // 2) * 2 + core, lax.rem(x, 2) * 4 + y)

    def step(v, by):
        return lax.rem(v + 4 + by, 4)

    x_img = x + 1 - 2 * odd
    x_txt = lax.rem(x + 3 + 2 * odd, 4)
    img_up = device(x, step(y, 1), z, core)
    img_down = device(x, step(y, -1), z, core)
    img_far = device(x, step(y, 2), z, core)
    img_side = device(x_img, y, z, core)
    txt_up = device(x, y, step(z, 1), core)
    txt_down = device(x, y, step(z, -1), core)
    txt_far = device(x, y, step(z, 2), core)
    txt_side = device(x_txt, y, z, core)
    twin = device(x, y, z, 1 - core)

    barrier = pltpu.get_barrier_semaphore()
    for peer in (img_up, img_down, img_far, img_side, txt_up, txt_down, txt_far, txt_side, twin):
        pl.semaphore_signal(barrier, inc=1, device_id=peer, device_id_type=MESH_ID)

    ti[0:ROWS] = unit_of(timg_raw[...])[0].astype(jnp.bfloat16)
    tt[0:ROWS] = unit_of(ttxt_raw[...])[0].astype(jnp.bfloat16)

    pl.semaphore_wait(barrier, 9)

    sent = []

    def remote(src, dst, ssem, rsem, dev):
        copy = pltpu.make_async_remote_copy(
            src_ref=src, dst_ref=dst, send_sem=ssem, recv_sem=rsem, device_id=dev, device_id_type=MESH_ID
        )
        copy.start()
        sent.append(copy)
        return copy

    img_devs = (img_up, img_down, img_side)
    txt_devs = (txt_up, txt_down, txt_side)
    arrays = {
        "ti": (ti, send_ti, recv_ti, ROWS, img_devs),
        "si": (si, send_si, recv_si, ROWS, img_devs),
        "tt": (tt, send_tt, recv_tt, 2 * ROWS, txt_devs),
        "st": (st, send_st, recv_st, 2 * ROWS, txt_devs),
    }
    got = {}
    UP, DOWN, SIDE = 0, 1, 2
    places = {
        "0": (0, 0, ROWS), "1": (1, 0, ROWS), "2": (2, 0, ROWS), "3": (3, 0, ROWS), "4": (4, 0, ROWS),
        "7": (5, 0, ROWS), "1b": (1, HALF, HALF), "2a": (2, 0, HALF), "3a": (3, 0, HALF), "3b": (3, HALF, HALF),
        "4a": (4, 0, HALF), "4b": (4, HALF, HALF),
        "5a": (6, 0, HALF), "6a": (6, HALF, HALF), "5b": (7, 0, HALF), "6b": (7, HALF, HALF),
    }
    index = {"1": 0, "2": 1, "3": 2, "4a": 3, "4b": 4, "7": 5, "5a": 6, "6a": 7, "5b": 8, "6b": 9}

    def hop(name, src, dst, way):
        ref, ssem, rsem, pitch, devs = arrays[name]
        s_slot, s_row, count = places[src]
        d_slot, d_row, _ = places[dst]
        got[name, dst] = remote(
            ref.at[pl.ds(s_slot * pitch + s_row, count)], ref.at[pl.ds(d_slot * pitch + d_row, count)],
            ssem.at[index[dst]], rsem.at[index[dst]], devs[way],
        )

    def across(name, slot):
        ref, _, _, pitch, _ = arrays[name]
        ssem, rsem = (csend_tt, crecv_tt) if name == "tt" else (csend_st, crecv_st)
        got[name + "c", slot] = remote(
            ref.at[pl.ds(slot * pitch, ROWS)], ref.at[pl.ds(slot * pitch + ROWS, ROWS)],
            ssem.at[slot], rsem.at[slot], twin,
        )

    def arrive(*keys):
        for key in keys:
            got[key].wait_recv()

    def first_hops(names):
        for name in names:
            hop(name, "0", "2", UP)
            hop(name, "0", "1", DOWN)
            hop(name, "0", "3", SIDE)

    first_hops(("ti", "tt"))
    across("tt", 0)
    si[0:ROWS] = unit_of(img_raw[...])[0].astype(jnp.bfloat16)
    st[0:ROWS] = unit_of(txt_raw[...])[0].astype(jnp.bfloat16)
    first_hops(("si", "st"))
    across("st", 0)

    def clear(i, _):
        rows = pl.ds(pl.multiple_of(i * ROWS, ROWS), ROWS)
        iacc[rows, :] = jnp.zeros((ROWS, iacc.shape[1]), jnp.float32)
        tacc[pl.ds(pl.multiple_of(i * 2 * ROWS, 2 * ROWS), 2 * ROWS), :] = jnp.zeros(
            (2 * ROWS, tacc.shape[1]), jnp.float32
        )
        return 0

    lax.fori_loop(0, 8, clear, 0)

    def teacher_value(zt):
        return 0.5 - 0.5 * jnp.tanh(half_scale * zt + half_bias)

    def columns(slot):
        return pl.ds(pl.multiple_of(slot * 2 * ROWS, 2 * ROWS), 2 * ROWS)

    def gradients(first, count, slot, teacher, diagonal):
        rows = slice(first, first + count)
        cols = columns(slot)
        zs = dot(si[rows], st[cols, :], NT)
        value = jnp.tanh(half_scale * zs + half_bias) + teacher
        if diagonal:
            row = lax.broadcasted_iota(jnp.int32, (ROWS, 2 * ROWS), 0)
            col = lax.broadcasted_iota(jnp.int32, (ROWS, 2 * ROWS), 1)
            positive = jnp.where(row == col + slot * 4 * ROWS, 1.0, 0.0)
            gs[0:ROWS] = (value[:ROWS] - positive).astype(jnp.bfloat16)
            gs[ROWS:count] = value[ROWS:].astype(jnp.bfloat16)
        else:
            gs[0:count] = value.astype(jnp.bfloat16)
        g = gs[0:count]
        iacc[rows] += dot(g, st[cols, :], NN)
        tacc[cols, :] += dot(g, si[rows], TN)

    def over(begin, end, one):
        lax.fori_loop(begin, end, lambda slot, _: (one(slot), 0)[1], 0)

    def whole(first, count, begin, end, diagonal=False):
        def one(slot):
            zt = dot(ti[first : first + count], tt[columns(slot), :], NT)
            gradients(first, count, slot, teacher_value(zt), diagonal)

        over(begin, end, one)

    def teach(first, count, begin, end):
        def one(slot):
            zt = dot(ti[first : first + count], tt[columns(slot), :], NT)
            ps[slot, first : first + count, :] = teacher_value(zt)

        over(begin, end, one)

    def learn(first, count, begin, end):
        def one(slot):
            gradients(first, count, slot, ps[slot, first : first + count, :], False)

        over(begin, end, one)

    def relay(names):
        for name in names:
            hop(name, "2a", "4a", UP)
            hop(name, "1b", "4b", DOWN)

    def to_ring(names):
        for half in "ab":
            for name in names:
                hop(name, "3" + half, "6" + half, UP)
                hop(name, "3" + half, "5" + half, DOWN)

    def second_hops(names):
        arrive(*[(name, part) for part in ("4a", "4b") for name in names])
        for name in names:
            hop(name, "4", "7", SIDE)
        across(names[1], 4)

    arrive(*[(name, part) for part in "123" for name in ("ti", "tt")])
    relay(("ti", "tt"))
    for slot in (1, 2, 3):
        across("tt", slot)
    arrive(*[(name, part) for part in "123" for name in ("si", "st")])
    relay(("si", "st"))
    to_ring(("ti", "tt"))
    to_ring(("si", "st"))
    for slot in (1, 2, 3):
        across("st", slot)

    arrive(*[(name, slot) for slot in range(4) for name in ("ttc", "stc")])
    whole(0, 512, 0, 2, True)
    second_hops(("ti", "tt"))
    whole(0, 512, 2, 4)
    second_hops(("si", "st"))
    whole(512, 128, 0, 4)
    arrive(("ttc", 4), ("stc", 4))
    whole(0, 640, 4, 5)

    arrive(("tt", "7"))
    across("tt", 5)
    arrive(("tt", "5a"), ("tt", "6a"))
    across("tt", 6)
    arrive(("tt", "5b"), ("tt", "6b"))
    across("tt", 7)
    arrive(*[("ti", part) for part in ("7", "5a", "6a", "5b", "6b")])
    teach(640, 384, 0, 5)
    arrive(("ttc", 5), ("ttc", 6), ("ttc", 7))
    teach(0, 1024, 5, 8)

    arrive(("st", "7"))
    across("st", 5)
    arrive(("st", "5a"), ("st", "6a"))
    across("st", 6)
    arrive(*[("si", part) for part in ("7", "5a", "6a")])
    learn(640, 256, 0, 5)
    arrive(("st", "5b"), ("st", "6b"))
    across("st", 7)
    arrive(("stc", 5), ("stc", 6))
    learn(0, 896, 5, 7)
    arrive(("si", "5b"), ("si", "6b"))
    learn(896, 128, 0, 7)

    def give(slots):
        for p in slots:
            lo = p * 2 * ROWS + ROWS
            tb[p * ROWS : (p + 1) * ROWS] = tacc[lo : lo + ROWS].astype(jnp.bfloat16)
        for p in slots:
            rows = pl.ds(p * ROWS, ROWS)
            got["g", p] = remote(tb.at[rows], crecv.at[rows], csend_g.at[p], crecv_g.at[p], twin)

    give((5, 1, 2, 6, 4, 3, 0))
    arrive(("stc", 7))
    learn(0, 1024, 7, 8)
    give((7,))

    def part_of(p, load):
        if p in (5, 6):
            lo = 0 if p == 5 else HALF
            return ((0, load(6, lo, HALF)), (HALF, load(7, lo, HALF)))
        return ((0, load(5 if p == 7 else p, 0, ROWS)),)

    def img_part(p):
        return part_of(p, lambda slot, lo, count: iacc[slot * ROWS + lo : slot * ROWS + lo + count])

    def txt_part(p):
        def load(slot, lo, count):
            mine = tacc[slot * 2 * ROWS + lo : slot * 2 * ROWS + lo + count]
            return mine + crecv[slot * ROWS + lo : slot * ROWS + lo + count].astype(jnp.float32)

        return part_of(p, load)

    def at(ref, p):
        return ref.at[pl.ds(p * ROWS, ROWS)]

    def fill(ref, p, parts):
        for lo, value in parts:
            ref[p * ROWS + lo : p * ROWS + lo + value.shape[0]] = value.astype(jnp.bfloat16)

    def put_img(p, slot, dev):
        got["i", slot] = remote(at(ib, p), at(irecv, slot), isend.at[slot], irsem.at[slot], dev)

    def put_txt(p, slot, dev):
        got["t", slot] = remote(at(ts, p), at(trecv, slot), tsend.at[slot], trsem.at[slot], dev)

    def came(ref, slot):
        return ref[slot * ROWS : (slot + 1) * ROWS].astype(jnp.float32)

    for p in (7, 5, 6, 1, 2):
        fill(ib, p, img_part(p))
    put_img(7, 0, img_side)
    put_img(5, 1, img_up)
    put_img(6, 2, img_down)
    put_img(1, 3, img_up)
    put_img(2, 4, img_down)
    arrive(*[("g", p) for p in (5, 1, 2)])
    for p in (7, 1, 2):
        fill(ts, p, txt_part(p))
    put_txt(7, 0, txt_side)
    put_txt(1, 3, txt_up)
    put_txt(2, 4, txt_down)
    arrive(*[("g", p) for p in (6, 4, 3, 0, 7)])
    for p in (5, 6):
        fill(ts, p, txt_part(p))
    put_txt(5, 1, txt_up)
    put_txt(6, 2, txt_down)

    arrive(("i", 0))
    ib[4 * ROWS : 5 * ROWS] = (iacc[4 * ROWS : 5 * ROWS] + came(irecv, 0)).astype(jnp.bfloat16)
    put_img(4, 5, img_far)
    arrive(("i", 1), ("i", 2))
    ib[3 * ROWS : 4 * ROWS] = (iacc[3 * ROWS : 4 * ROWS] + came(irecv, 1) + came(irecv, 2)).astype(jnp.bfloat16)
    put_img(3, 6, img_side)
    arrive(("t", 0))
    ts[4 * ROWS : 5 * ROWS] = (txt_part(4)[0][1] + came(trecv, 0)).astype(jnp.bfloat16)
    put_txt(4, 5, txt_far)
    arrive(("t", 1), ("t", 2))
    ts[3 * ROWS : 4 * ROWS] = (txt_part(3)[0][1] + came(trecv, 1) + came(trecv, 2)).astype(jnp.bfloat16)
    put_txt(3, 6, txt_side)

    arrive(*[("i", slot) for slot in (3, 4, 5, 6)])
    total = iacc[0:ROWS] + came(irecv, 3) + came(irecv, 4) + came(irecv, 5) + came(irecv, 6)
    image_grad[...] = back(logit_scale * total, img_raw[...])
    arrive(*[("t", slot) for slot in (3, 4, 5, 6)])
    total = txt_part(0)[0][1] + came(trecv, 3) + came(trecv, 4) + came(trecv, 5) + came(trecv, 6)
    text_grad[...] = back(logit_scale * total, txt_raw[...])

    for copy in sent:
        copy.wait_send()


def body(student_img, student_txt, teacher_img, teacher_txt):
    width = student_img.shape[1]
    t_width = teacher_img.shape[1]
    bf16, f32 = jnp.bfloat16, jnp.float32
    vmem = pl.BlockSpec(memory_space=pltpu.VMEM)
    dma = pltpu.SemaphoreType.DMA((10,))
    return pl.pallas_call(
        kernel,
        out_shape=[jax.ShapeDtypeStruct((ROWS, width), f32)] * 2,
        in_specs=[vmem] * 4,
        out_specs=[vmem] * 2,
        scratch_shapes=[
            pltpu.VMEM((8 * ROWS, width), bf16),
            pltpu.VMEM((8 * ROWS, t_width), bf16),
            pltpu.VMEM((16 * ROWS, width), bf16),
            pltpu.VMEM((16 * ROWS, t_width), bf16),
            pltpu.VMEM((8, 8 * ROWS, 2 * ROWS), f32),
            pltpu.VMEM((8 * ROWS, 2 * ROWS), bf16),
            pltpu.VMEM((8 * ROWS, width), f32),
            pltpu.VMEM((16 * ROWS, width), f32),
            pltpu.VMEM((8 * ROWS, width), bf16),
            pltpu.VMEM((8 * ROWS, width), bf16),
            pltpu.VMEM((8 * ROWS, width), bf16),
            pltpu.VMEM((8 * ROWS, width), bf16),
            pltpu.VMEM((7 * ROWS, width), bf16),
            pltpu.VMEM((7 * ROWS, width), bf16),
        ]
        + [dma] * 18,
        compiler_params=pltpu.CompilerParams(
            collective_id=0, has_side_effects=True, vmem_limit_bytes=62 << 20
        ),
    )(student_img, student_txt, teacher_img, teacher_txt)


def solution(mesh):
    rows = P(("blk", "narrow"), None)
    return jax.shard_map(body, mesh=mesh, in_specs=(rows,) * 4, out_specs=(rows, rows), check_vma=False)
```

time: 100 us -> 106 us (1.060)
  Pallas kernels: 96.2 us -> 102 us
    pallas_call x1, Pallas kernels: 96.2 us -> 102 us  [body(): pl.pallas_call(kernel, out_shape=[jax.ShapeDtypeStruct((ROWS, width), f32...]
where the time goes in v2:
time: 106 us
  Pallas kernels  102 us (96%)
  local copies, waits for them, and re-layouts  2.8 us (3%)
    pallas_call x1, Pallas kernels, body(): pl.pallas_call(kernel, out_shape=[jax.ShapeDtypeStruct((ROWS, width), f32...  102 us
    unnamed x4, local copies, waits for them, and re-layouts  2.8 us

profile of v2, /device:TPU:0, one launch (start us, length us, event | category | flops | bytes accessed | tf_op | source)
XLA Modules:
  0.0 105.9 jit_solution(13825046368840433114)
XLA Ops:
  0.6 102.5 %shard_map.59 = (f32[128,1152]{1,0:T(8,128)}, f32[128,1152]{1,0:T(8,128)}) custom-call(bf16[128,1152]{1,0:T(8,128)(2,1)} %img_raw.1, bf16[128,1152]{1,0:T(8,128)(2,1)} %txt_raw.1, bf16[128,1536]{1,0:T(8,128)(2,1)} %timg_raw.1, bf16[128,1536]{1,0:T(8,128)(2,1)} %ttxt_raw.1), custom_call_target="tpu_custom_call" | custom-call | tf_op jit(solution)/shard_map/pallas_call | solution.py:353
  103.1 0.0 copy-start
  103.1 2.0 %copy.8 = f32[128,1152]{1,0:T(8,128)} copy(f32[128,1152]{1,0:T(8,128)} %get-tuple-element.4) | data formatting | bytes 1179648
  105.1 0.0 copy-done
  105.1 0.8 copy.9
Async XLA Ops:
  103.1 2.0 %copy-start = (f32[128,1152]{1,0:T(8,128)S(1)}, f32[128,1152]{1,0:T(8,128)}, u32[]{:S(2)}) copy-start(f32[128,1152]{1,0:T(8,128)} %get-tuple-element.5) | copy-start | bytes 1769476

commit v3 on v2

--- a/solution.py
+++ b/solution.py
@@ -38,7 +38,7 @@
 
 def kernel(
     img_raw, txt_raw, timg_raw, ttxt_raw, image_grad, text_grad,
-    si, ti, st, tt, ps, gs, iacc, tacc, ib, tb, ts, crecv, irecv, trecv,
+    si, ti, st, tt, pn2, pa2, pn3, pa3, gs, iacc, tacc, ib, tb, ts, crecv, irecv, trecv,
     send_si, send_ti, send_st, send_tt, recv_si, recv_ti, recv_st, recv_tt,
     csend_st, csend_tt, crecv_st, crecv_tt, csend_g, crecv_g, isend, irsem, tsend, trsem,
 ):
@@ -97,13 +97,13 @@
     }
     got = {}
     UP, DOWN, SIDE = 0, 1, 2
-    places = {
-        "0": (0, 0, ROWS), "1": (1, 0, ROWS), "2": (2, 0, ROWS), "3": (3, 0, ROWS), "4": (4, 0, ROWS),
-        "7": (5, 0, ROWS), "1b": (1, HALF, HALF), "2a": (2, 0, HALF), "3a": (3, 0, HALF), "3b": (3, HALF, HALF),
-        "4a": (4, 0, HALF), "4b": (4, HALF, HALF),
-        "5a": (6, 0, HALF), "6a": (6, HALF, HALF), "5b": (7, 0, HALF), "6b": (7, HALF, HALF),
-    }
-    index = {"1": 0, "2": 1, "3": 2, "4a": 3, "4b": 4, "7": 5, "5a": 6, "6a": 7, "5b": 8, "6b": 9}
+    slot_of = {"0": 0, "1": 1, "2": 2, "3": 3, "4": 4, "7": 5, "5": 6, "6": 7}
+    places = {}
+    for chip, slot in slot_of.items():
+        places[chip] = (slot, 0, ROWS)
+        places[chip + "a"] = (slot, 0, HALF)
+        places[chip + "b"] = (slot, HALF, HALF)
+    index = {k: i for i, k in enumerate(("1a", "1b", "2a", "2b", "3", "4a", "4b", "7", "5", "6"))}
 
     def hop(name, src, dst, way):
         ref, ssem, rsem, pitch, devs = arrays[name]
@@ -126,18 +126,24 @@
         for key in keys:
             got[key].wait_recv()
 
-    def first_hops(names):
-        for name in names:
-            hop(name, "0", "2", UP)
-            hop(name, "0", "1", DOWN)
+    def to_ring_first(names):
+        for name in names:
+            hop(name, "0a", "2a", UP)
+            hop(name, "0b", "1b", DOWN)
+        for name in names:
+            hop(name, "0b", "2b", UP)
+            hop(name, "0a", "1a", DOWN)
+
+    def to_side_first(names):
+        for name in names:
             hop(name, "0", "3", SIDE)
-
-    first_hops(("ti", "tt"))
-    across("tt", 0)
+        across(names[1], 0)
+
+    to_ring_first(("ti", "tt"))
+    to_side_first(("ti", "tt"))
     si[0:ROWS] = unit_of(img_raw[...])[0].astype(jnp.bfloat16)
     st[0:ROWS] = unit_of(txt_raw[...])[0].astype(jnp.bfloat16)
-    first_hops(("si", "st"))
-    across("st", 0)
+    to_side_first(("si", "st"))
 
     def clear(i, _):
         rows = pl.ds(pl.multiple_of(i * ROWS, ROWS), ROWS)
@@ -152,18 +158,22 @@
     def teacher_value(zt):
         return 0.5 - 0.5 * jnp.tanh(half_scale * zt + half_bias)
 
-    def columns(slot):
-        return pl.ds(pl.multiple_of(slot * 2 * ROWS, 2 * ROWS), 2 * ROWS)
-
-    def gradients(first, count, slot, teacher, diagonal):
+    WIDE = 4 * ROWS
+
+    def columns(pair):
+        return pl.ds(pl.multiple_of(pair * WIDE, WIDE), WIDE)
+
+    def teach(first, count, pair):
+        return teacher_value(dot(ti[first : first + count], tt[columns(pair), :], NT))
+
+    def learn(first, count, pair, teacher, diagonal=False):
         rows = slice(first, first + count)
-        cols = columns(slot)
-        zs = dot(si[rows], st[cols, :], NT)
-        value = jnp.tanh(half_scale * zs + half_bias) + teacher
+        cols = columns(pair)
+        value = jnp.tanh(half_scale * dot(si[rows], st[cols, :], NT) + half_bias) + teacher
         if diagonal:
-            row = lax.broadcasted_iota(jnp.int32, (ROWS, 2 * ROWS), 0)
-            col = lax.broadcasted_iota(jnp.int32, (ROWS, 2 * ROWS), 1)
-            positive = jnp.where(row == col + slot * 4 * ROWS, 1.0, 0.0)
+            row = lax.broadcasted_iota(jnp.int32, (ROWS, WIDE), 0)
+            col = lax.broadcasted_iota(jnp.int32, (ROWS, WIDE), 1)
+            positive = jnp.where(row == col + pair * WIDE, 1.0, 0.0)
             gs[0:ROWS] = (value[:ROWS] - positive).astype(jnp.bfloat16)
             gs[ROWS:count] = value[ROWS:].astype(jnp.bfloat16)
         else:
@@ -173,88 +183,79 @@
         tacc[cols, :] += dot(g, si[rows], TN)
 
     def over(begin, end, one):
-        lax.fori_loop(begin, end, lambda slot, _: (one(slot), 0)[1], 0)
-
-    def whole(first, count, begin, end, diagonal=False):
-        def one(slot):
-            zt = dot(ti[first : first + count], tt[columns(slot), :], NT)
-            gradients(first, count, slot, teacher_value(zt), diagonal)
-
-        over(begin, end, one)
-
-    def teach(first, count, begin, end):
-        def one(slot):
-            zt = dot(ti[first : first + count], tt[columns(slot), :], NT)
-            ps[slot, first : first + count, :] = teacher_value(zt)
-
-        over(begin, end, one)
-
-    def learn(first, count, begin, end):
-        def one(slot):
-            gradients(first, count, slot, ps[slot, first : first + count, :], False)
-
-        over(begin, end, one)
+        lax.fori_loop(begin, end, lambda pair, _: (one(pair), 0)[1], 0)
 
     def relay(names):
+        arrive(*[(name, part) for part in ("2a", "1b") for name in names])
         for name in names:
             hop(name, "2a", "4a", UP)
             hop(name, "1b", "4b", DOWN)
 
     def to_ring(names):
-        for half in "ab":
-            for name in names:
-                hop(name, "3" + half, "6" + half, UP)
-                hop(name, "3" + half, "5" + half, DOWN)
-
-    def second_hops(names):
+        for name in names:
+            hop(name, "3", "6", UP)
+            hop(name, "3", "5", DOWN)
+
+    def near_across(names):
+        arrive(*[(name, part) for part in ("2b", "1a", "3") for name in names])
+        for slot in (1, 2, 3):
+            across(names[1], slot)
+
+    def far_to_side(names):
         arrive(*[(name, part) for part in ("4a", "4b") for name in names])
         for name in names:
             hop(name, "4", "7", SIDE)
         across(names[1], 4)
 
-    arrive(*[(name, part) for part in "123" for name in ("ti", "tt")])
-    relay(("ti", "tt"))
-    for slot in (1, 2, 3):
-        across("tt", slot)
-    arrive(*[(name, part) for part in "123" for name in ("si", "st")])
-    relay(("si", "st"))
-    to_ring(("ti", "tt"))
-    to_ring(("si", "st"))
-    for slot in (1, 2, 3):
-        across("st", slot)
+    def late_across(name, chips):
+        for chip in chips:
+            arrive((name, chip))
+            across(name, slot_of[chip])
+
+    TEACHER, STUDENT = ("ti", "tt"), ("si", "st")
+    relay(TEACHER)
+    to_ring_first(STUDENT)
+    near_across(TEACHER)
+    far_to_side(TEACHER)
+    relay(STUDENT)
+    to_ring(TEACHER)
+    near_across(STUDENT)
+    to_ring(STUDENT)
 
     arrive(*[(name, slot) for slot in range(4) for name in ("ttc", "stc")])
-    whole(0, 512, 0, 2, True)
-    second_hops(("ti", "tt"))
-    whole(0, 512, 2, 4)
-    second_hops(("si", "st"))
-    whole(512, 128, 0, 4)
-    arrive(("ttc", 4), ("stc", 4))
-    whole(0, 640, 4, 5)
-
-    arrive(("tt", "7"))
-    across("tt", 5)
-    arrive(("tt", "5a"), ("tt", "6a"))
-    across("tt", 6)
-    arrive(("tt", "5b"), ("tt", "6b"))
-    across("tt", 7)
-    arrive(*[("ti", part) for part in ("7", "5a", "6a", "5b", "6b")])
-    teach(640, 384, 0, 5)
-    arrive(("ttc", 5), ("ttc", 6), ("ttc", 7))
-    teach(0, 1024, 5, 8)
-
-    arrive(("st", "7"))
-    across("st", 5)
-    arrive(("st", "5a"), ("st", "6a"))
-    across("st", 6)
-    arrive(*[("si", part) for part in ("7", "5a", "6a")])
-    learn(640, 256, 0, 5)
-    arrive(("st", "5b"), ("st", "6b"))
-    across("st", 7)
-    arrive(("stc", 5), ("stc", 6))
-    learn(0, 896, 5, 7)
-    arrive(("si", "5b"), ("si", "6b"))
-    learn(896, 128, 0, 7)
+    learn(0, 512, 0, teach(0, 512, 0), True)
+    far_to_side(STUDENT)
+    learn(0, 512, 1, teach(0, 512, 1))
+
+    late_across("tt", "7")
+    arrive(("ti", "7"))
+
+    def teach_new2(pair):
+        pn2[pair] = teach(512, 256, pair)
+
+    over(0, 2, teach_new2)
+    arrive(("ttc", 4), ("ttc", 5))
+    pa2[...] = teach(0, 768, 2)
+
+    late_across("st", "7")
+    arrive(("si", "7"))
+    over(0, 2, lambda pair: learn(512, 256, pair, pn2[pair]))
+    arrive(("stc", 4), ("stc", 5))
+    learn(0, 768, 2, pa2[...])
+
+    late_across("tt", "56")
+    arrive(("ti", "5"), ("ti", "6"))
+
+    def teach_new3(pair):
+        pn3[pair] = teach(768, 256, pair)
+
+    over(0, 3, teach_new3)
+    arrive(("ttc", 6), ("ttc", 7))
+    pa3[...] = teach(0, 1024, 3)
+
+    late_across("st", "56")
+    arrive(("si", "5"), ("si", "6"))
+    over(0, 3, lambda pair: learn(768, 256, pair, pn3[pair]))
 
     def give(slots):
         for p in slots:
@@ -264,33 +265,25 @@
             rows = pl.ds(p * ROWS, ROWS)
             got["g", p] = remote(tb.at[rows], crecv.at[rows], csend_g.at[p], crecv_g.at[p], twin)
 
-    give((5, 1, 2, 6, 4, 3, 0))
-    arrive(("stc", 7))
-    learn(0, 1024, 7, 8)
-    give((7,))
-
-    def part_of(p, load):
-        if p in (5, 6):
-            lo = 0 if p == 5 else HALF
-            return ((0, load(6, lo, HALF)), (HALF, load(7, lo, HALF)))
-        return ((0, load(5 if p == 7 else p, 0, ROWS)),)
+    give((5, 1, 2, 4, 3, 0))
+    arrive(("stc", 6), ("stc", 7))
+    learn(0, 1024, 3, pa3[...])
+    give((6, 7))
 
     def img_part(p):
-        return part_of(p, lambda slot, lo, count: iacc[slot * ROWS + lo : slot * ROWS + lo + count])
+        slot = slot_of[str(p)]
+        return iacc[slot * ROWS : (slot + 1) * ROWS]
 
     def txt_part(p):
-        def load(slot, lo, count):
-            mine = tacc[slot * 2 * ROWS + lo : slot * 2 * ROWS + lo + count]
-            return mine + crecv[slot * ROWS + lo : slot * ROWS + lo + count].astype(jnp.float32)
-
-        return part_of(p, load)
+        slot = slot_of[str(p)]
+        mine = tacc[slot * 2 * ROWS : slot * 2 * ROWS + ROWS]
+        return mine + crecv[slot * ROWS : (slot + 1) * ROWS].astype(jnp.float32)
 
     def at(ref, p):
         return ref.at[pl.ds(p * ROWS, ROWS)]
 
-    def fill(ref, p, parts):
-        for lo, value in parts:
-            ref[p * ROWS + lo : p * ROWS + lo + value.shape[0]] = value.astype(jnp.bfloat16)
+    def fill(ref, p, value):
+        ref[p * ROWS : (p + 1) * ROWS] = value.astype(jnp.bfloat16)
 
     def put_img(p, slot, dev):
         got["i", slot] = remote(at(ib, p), at(irecv, slot), isend.at[slot], irsem.at[slot], dev)
@@ -314,7 +307,7 @@
     put_txt(7, 0, txt_side)
     put_txt(1, 3, txt_up)
     put_txt(2, 4, txt_down)
-    arrive(*[("g", p) for p in (6, 4, 3, 0, 7)])
+    arrive(*[("g", p) for p in (4, 3, 0, 6, 7)])
     for p in (5, 6):
         fill(ts, p, txt_part(p))
     put_txt(5, 1, txt_up)
@@ -327,17 +320,17 @@
     ib[3 * ROWS : 4 * ROWS] = (iacc[3 * ROWS : 4 * ROWS] + came(irecv, 1) + came(irecv, 2)).astype(jnp.bfloat16)
     put_img(3, 6, img_side)
     arrive(("t", 0))
-    ts[4 * ROWS : 5 * ROWS] = (txt_part(4)[0][1] + came(trecv, 0)).astype(jnp.bfloat16)
+    ts[4 * ROWS : 5 * ROWS] = (txt_part(4) + came(trecv, 0)).astype(jnp.bfloat16)
     put_txt(4, 5, txt_far)
     arrive(("t", 1), ("t", 2))
-    ts[3 * ROWS : 4 * ROWS] = (txt_part(3)[0][1] + came(trecv, 1) + came(trecv, 2)).astype(jnp.bfloat16)
+    ts[3 * ROWS : 4 * ROWS] = (txt_part(3) + came(trecv, 1) + came(trecv, 2)).astype(jnp.bfloat16)
     put_txt(3, 6, txt_side)
 
     arrive(*[("i", slot) for slot in (3, 4, 5, 6)])
     total = iacc[0:ROWS] + came(irecv, 3) + came(irecv, 4) + came(irecv, 5) + came(irecv, 6)
     image_grad[...] = back(logit_scale * total, img_raw[...])
     arrive(*[("t", slot) for slot in (3, 4, 5, 6)])
-    total = txt_part(0)[0][1] + came(trecv, 3) + came(trecv, 4) + came(trecv, 5) + came(trecv, 6)
+    total = txt_part(0) + came(trecv, 3) + came(trecv, 4) + came(trecv, 5) + came(trecv, 6)
     text_grad[...] = back(logit_scale * total, txt_raw[...])
 
     for copy in sent:
@@ -360,8 +353,11 @@
             pltpu.VMEM((8 * ROWS, t_width), bf16),
             pltpu.VMEM((16 * ROWS, width), bf16),
             pltpu.VMEM((16 * ROWS, t_width), bf16),
-            pltpu.VMEM((8, 8 * ROWS, 2 * ROWS), f32),
-            pltpu.VMEM((8 * ROWS, 2 * ROWS), bf16),
+            pltpu.VMEM((2, 2 * ROWS, 4 * ROWS), f32),
+            pltpu.VMEM((6 * ROWS, 4 * ROWS), f32),
+            pltpu.VMEM((3, 2 * ROWS, 4 * ROWS), f32),
+            pltpu.VMEM((8 * ROWS, 4 * ROWS), f32),
+            pltpu.VMEM((8 * ROWS, 4 * ROWS), bf16),
             pltpu.VMEM((8 * ROWS, width), f32),
             pltpu.VMEM((16 * ROWS, width), f32),
             pltpu.VMEM((8 * ROWS, width), bf16),

time: 106 us -> 96.5 us (0.910)
  Pallas kernels: 102 us -> 92.9 us
    pallas_call x1, Pallas kernels: 102 us -> 92.9 us  [body(): pl.pallas_call(kernel, out_shape=[jax.ShapeDtypeStruct((ROWS, width), f32...]
where the time goes in v3:
time: 96.5 us; the launch traced here: 96.3 us
  Pallas kernels  92.9 us (96%)
  local copies, waits for them, and re-layouts  2.8 us (3%)
    pallas_call x1, Pallas kernels, body(): pl.pallas_call(kernel, out_shape=[jax.ShapeDtypeStruct((ROWS, width), f32...  92.9 us
    unnamed x4, local copies, waits for them, and re-layouts  2.8 us

profile of v3, /device:TPU:0, one launch (start us, length us, event | category | flops | bytes accessed | tf_op | source)
XLA Modules:
  0.0 96.3 jit_solution(3226693123877462891)
XLA Ops:
  0.6 92.9 %shard_map.59 = (f32[128,1152]{1,0:T(8,128)}, f32[128,1152]{1,0:T(8,128)}) custom-call(bf16[128,1152]{1,0:T(8,128)(2,1)} %img_raw.1, bf16[128,1152]{1,0:T(8,128)(2,1)} %txt_raw.1, bf16[128,1536]{1,0:T(8,128)(2,1)} %timg_raw.1, bf16[128,1536]{1,0:T(8,128)(2,1)} %ttxt_raw.1), custom_call_target="tpu_custom_call" | custom-call | tf_op jit(solution)/shard_map/pallas_call | solution.py:346
  93.5 0.0 copy-start
  93.5 2.0 %copy.8 = f32[128,1152]{1,0:T(8,128)} copy(f32[128,1152]{1,0:T(8,128)} %get-tuple-element.4) | data formatting | bytes 1179648
  95.5 0.0 copy-done
  95.5 0.8 copy.9
Async XLA Ops:
  93.5 2.0 %copy-start = (f32[128,1152]{1,0:T(8,128)S(1)}, f32[128,1152]{1,0:T(8,128)}, u32[]{:S(2)}) copy-start(f32[128,1152]{1,0:T(8,128)} %get-tuple-element.5) | copy-start | bytes 1769476

commit v4 on v3

--- a/solution.py
+++ b/solution.py
@@ -37,10 +37,10 @@
 
 
 def kernel(
-    img_raw, txt_raw, timg_raw, ttxt_raw, image_grad, text_grad,
+    img_hbm, txt_hbm, timg_hbm, ttxt_hbm, image_grad, text_grad, img_raw, txt_raw, timg_raw, ttxt_raw,
     si, ti, st, tt, pn2, pa2, pn3, pa3, gs, iacc, tacc, ib, tb, ts, crecv, irecv, trecv,
     send_si, send_ti, send_st, send_tt, recv_si, recv_ti, recv_st, recv_tt,
-    csend_st, csend_tt, crecv_st, crecv_tt, csend_g, crecv_g, isend, irsem, tsend, trsem,
+    csend_st, csend_tt, crecv_st, crecv_tt, csend_g, crecv_g, load, isend, irsem, tsend, trsem,
 ):
     b = lax.axis_index("blk")
     n = lax.axis_index("narrow")
@@ -60,22 +60,30 @@
     x_txt = lax.rem(x + 3 + 2 * odd, 4)
     img_up = device(x, step(y, 1), z, core)
     img_down = device(x, step(y, -1), z, core)
-    img_far = device(x, step(y, 2), z, core)
     img_side = device(x_img, y, z, core)
     txt_up = device(x, y, step(z, 1), core)
     txt_down = device(x, y, step(z, -1), core)
-    txt_far = device(x, y, step(z, 2), core)
     txt_side = device(x_txt, y, z, core)
     twin = device(x, y, z, 1 - core)
 
     barrier = pltpu.get_barrier_semaphore()
-    for peer in (img_up, img_down, img_far, img_side, txt_up, txt_down, txt_far, txt_side, twin):
+    for peer in (img_up, img_down, img_side, txt_up, txt_down, txt_side, twin):
         pl.semaphore_signal(barrier, inc=1, device_id=peer, device_id_type=MESH_ID)
 
+    loads = [
+        pltpu.make_async_copy(src, dst, load.at[i])
+        for i, (src, dst) in enumerate(
+            ((timg_hbm, timg_raw), (ttxt_hbm, ttxt_raw), (img_hbm, img_raw), (txt_hbm, txt_raw))
+        )
+    ]
+    for copy in loads:
+        copy.start()
+    for copy in loads[:2]:
+        copy.wait()
     ti[0:ROWS] = unit_of(timg_raw[...])[0].astype(jnp.bfloat16)
     tt[0:ROWS] = unit_of(ttxt_raw[...])[0].astype(jnp.bfloat16)
 
-    pl.semaphore_wait(barrier, 9)
+    pl.semaphore_wait(barrier, 7)
 
     sent = []
 
@@ -97,7 +105,7 @@
     }
     got = {}
     UP, DOWN, SIDE = 0, 1, 2
-    slot_of = {"0": 0, "1": 1, "2": 2, "3": 3, "4": 4, "7": 5, "5": 6, "6": 7}
+    slot_of = {"0": 0, "3": 1, "1": 2, "2": 3, "4": 4, "7": 5, "5": 6, "6": 7}
     places = {}
     for chip, slot in slot_of.items():
         places[chip] = (slot, 0, ROWS)
@@ -141,6 +149,8 @@
 
     to_ring_first(("ti", "tt"))
     to_side_first(("ti", "tt"))
+    for copy in loads[2:]:
+        copy.wait()
     si[0:ROWS] = unit_of(img_raw[...])[0].astype(jnp.bfloat16)
     st[0:ROWS] = unit_of(txt_raw[...])[0].astype(jnp.bfloat16)
     to_side_first(("si", "st"))
@@ -205,7 +215,7 @@
         arrive(*[(name, part) for part in ("4a", "4b") for name in names])
         for name in names:
             hop(name, "4", "7", SIDE)
-        across(names[1], 4)
+        across(names[1], slot_of["4"])
 
     def late_across(name, chips):
         for chip in chips:
@@ -255,8 +265,6 @@
 
     late_across("st", "56")
     arrive(("si", "5"), ("si", "6"))
-    over(0, 3, lambda pair: learn(768, 256, pair, pn3[pair]))
-
     def give(slots):
         for p in slots:
             lo = p * 2 * ROWS + ROWS
@@ -265,73 +273,116 @@
             rows = pl.ds(p * ROWS, ROWS)
             got["g", p] = remote(tb.at[rows], crecv.at[rows], csend_g.at[p], crecv_g.at[p], twin)
 
-    give((5, 1, 2, 4, 3, 0))
-    arrive(("stc", 6), ("stc", 7))
-    learn(0, 1024, 3, pa3[...])
-    give((6, 7))
-
-    def img_part(p):
-        slot = slot_of[str(p)]
+    def img_part(chip):
+        slot = slot_of[chip]
         return iacc[slot * ROWS : (slot + 1) * ROWS]
 
-    def txt_part(p):
-        slot = slot_of[str(p)]
+    def txt_part(chip):
+        slot = slot_of[chip]
         mine = tacc[slot * 2 * ROWS : slot * 2 * ROWS + ROWS]
         return mine + crecv[slot * ROWS : (slot + 1) * ROWS].astype(jnp.float32)
 
-    def at(ref, p):
-        return ref.at[pl.ds(p * ROWS, ROWS)]
-
-    def fill(ref, p, value):
-        ref[p * ROWS : (p + 1) * ROWS] = value.astype(jnp.bfloat16)
-
-    def put_img(p, slot, dev):
-        got["i", slot] = remote(at(ib, p), at(irecv, slot), isend.at[slot], irsem.at[slot], dev)
-
-    def put_txt(p, slot, dev):
-        got["t", slot] = remote(at(ts, p), at(trecv, slot), tsend.at[slot], trsem.at[slot], dev)
-
-    def came(ref, slot):
-        return ref[slot * ROWS : (slot + 1) * ROWS].astype(jnp.float32)
-
-    for p in (7, 5, 6, 1, 2):
-        fill(ib, p, img_part(p))
-    put_img(7, 0, img_side)
-    put_img(5, 1, img_up)
-    put_img(6, 2, img_down)
-    put_img(1, 3, img_up)
-    put_img(2, 4, img_down)
-    arrive(*[("g", p) for p in (5, 1, 2)])
-    for p in (7, 1, 2):
-        fill(ts, p, txt_part(p))
-    put_txt(7, 0, txt_side)
-    put_txt(1, 3, txt_up)
-    put_txt(2, 4, txt_down)
-    arrive(*[("g", p) for p in (4, 3, 0, 6, 7)])
-    for p in (5, 6):
-        fill(ts, p, txt_part(p))
-    put_txt(5, 1, txt_up)
-    put_txt(6, 2, txt_down)
-
-    arrive(("i", 0))
-    ib[4 * ROWS : 5 * ROWS] = (iacc[4 * ROWS : 5 * ROWS] + came(irecv, 0)).astype(jnp.bfloat16)
-    put_img(4, 5, img_far)
-    arrive(("i", 1), ("i", 2))
-    ib[3 * ROWS : 4 * ROWS] = (iacc[3 * ROWS : 4 * ROWS] + came(irecv, 1) + came(irecv, 2)).astype(jnp.bfloat16)
-    put_img(3, 6, img_side)
-    arrive(("t", 0))
-    ts[4 * ROWS : 5 * ROWS] = (txt_part(4) + came(trecv, 0)).astype(jnp.bfloat16)
-    put_txt(4, 5, txt_far)
-    arrive(("t", 1), ("t", 2))
-    ts[3 * ROWS : 4 * ROWS] = (txt_part(3) + came(trecv, 1) + came(trecv, 2)).astype(jnp.bfloat16)
-    put_txt(3, 6, txt_side)
-
-    arrive(*[("i", slot) for slot in (3, 4, 5, 6)])
-    total = iacc[0:ROWS] + came(irecv, 3) + came(irecv, 4) + came(irecv, 5) + came(irecv, 6)
-    image_grad[...] = back(logit_scale * total, img_raw[...])
-    arrive(*[("t", slot) for slot in (3, 4, 5, 6)])
-    total = txt_part(0) + came(trecv, 3) + came(trecv, 4) + came(trecv, 5) + came(trecv, 6)
-    text_grad[...] = back(logit_scale * total, txt_raw[...])
+    part = {"i": img_part, "t": txt_part}
+    out_buf = {"i": ib, "t": ts}
+    in_buf = {"i": irecv, "t": trecv}
+    out_sem = {"i": isend, "t": tsend}
+    in_sem = {"i": irsem, "t": trsem}
+    peers = {"i": img_devs, "t": txt_devs}
+    piece = {"1": (0, ROWS, 0), "2": (ROWS, ROWS, 1), "3": (2 * ROWS, ROWS, 2), "4": (3 * ROWS, ROWS, 3),
+             "5": (4 * ROWS, ROWS, 4), "6": (5 * ROWS, ROWS, 5), "7": (6 * ROWS, ROWS, 6)}
+    for chip, first_sem in (("1", 0), ("2", 1), ("4", 3)):
+        row = piece[chip][0]
+        piece[chip + "a"] = (row, HALF, first_sem)
+        piece[chip + "b"] = (row + HALF, HALF, first_sem + 7 if chip != "4" else 9)
+
+    def rows_of(ref, key):
+        row, count, _ = piece[key]
+        return ref[row : row + count]
+
+    def fill(stream, key, value):
+        row, count, _ = piece[key]
+        out_buf[stream][row : row + count] = value.astype(jnp.bfloat16)
+
+    def put(stream, key, way):
+        row, count, sem = piece[key]
+        rows = pl.ds(row, count)
+        got[stream, "sum" + key] = remote(
+            out_buf[stream].at[rows], in_buf[stream].at[rows],
+            out_sem[stream].at[sem], in_sem[stream].at[sem], peers[stream][way],
+        )
+
+    def came(stream, key):
+        arrive((stream, "sum" + key))
+        return rows_of(in_buf[stream], key).astype(jnp.float32)
+
+    def send_7(stream):
+        fill(stream, "7", part[stream]("7"))
+        put(stream, "7", SIDE)
+
+    def send_near(stream):
+        fill(stream, "1", part[stream]("1"))
+        fill(stream, "2", part[stream]("2"))
+        put(stream, "1a", UP)
+        put(stream, "2b", DOWN)
+
+    def send_56(stream):
+        fill(stream, "5", part[stream]("5"))
+        fill(stream, "6", part[stream]("6"))
+        put(stream, "5", UP)
+        put(stream, "6", DOWN)
+
+    def send_far(stream):
+        fill(stream, "4", part[stream]("4") + came(stream, "7"))
+        put(stream, "4b", UP)
+        put(stream, "4a", DOWN)
+
+    def send_side(stream):
+        fill(stream, "3", part[stream]("3") + came(stream, "5") + came(stream, "6"))
+        put(stream, "3", SIDE)
+
+    def send_rest(stream):
+        fill(stream, "1b", part[stream]("1")[HALF:] + came(stream, "4b"))
+        fill(stream, "2a", part[stream]("2")[:HALF] + came(stream, "4a"))
+        put(stream, "1b", UP)
+        put(stream, "2a", DOWN)
+
+    def total(stream):
+        for key in ("1a", "1b", "2a", "2b"):
+            arrive((stream, "sum" + key))
+        near = rows_of(in_buf[stream], "1").astype(jnp.float32) + rows_of(in_buf[stream], "2").astype(jnp.float32)
+        return logit_scale * (part[stream]("0") + near + came(stream, "3"))
+
+    learn(768, 256, 2, pn3[2])
+    give((5, 4))
+    learn(768, 256, 1, pn3[1])
+    give((2, 3))
+    arrive(("stc", 6), ("stc", 7))
+    learn(512, 256, 3, pa3[512:768])
+    arrive(("g", 5))
+    send_7("i")
+    send_7("t")
+    learn(0, 512, 3, pa3[0:512])
+    send_near("i")
+    arrive(("g", 2), ("g", 3))
+    send_near("t")
+    learn(768, 256, 3, pa3[768:1024])
+    give((6, 7))
+    learn(768, 256, 0, pn3[0])
+    send_56("i")
+    arrive(("g", 6), ("g", 7))
+    send_56("t")
+    give((1, 0))
+    arrive(("g", 4))
+    send_far("i")
+    send_far("t")
+    arrive(("g", 1))
+    send_side("i")
+    send_side("t")
+    send_rest("i")
+    send_rest("t")
+    image_grad[...] = back(total("i"), img_raw[...])
+    arrive(("g", 0))
+    text_grad[...] = back(total("t"), txt_raw[...])
 
     for copy in sent:
         copy.wait_send()
@@ -346,9 +397,13 @@
     return pl.pallas_call(
         kernel,
         out_shape=[jax.ShapeDtypeStruct((ROWS, width), f32)] * 2,
-        in_specs=[vmem] * 4,
+        in_specs=[pl.BlockSpec(memory_space=pl.ANY)] * 4,
         out_specs=[vmem] * 2,
         scratch_shapes=[
+            pltpu.VMEM((ROWS, width), bf16),
+            pltpu.VMEM((ROWS, width), bf16),
+            pltpu.VMEM((ROWS, t_width), bf16),
+            pltpu.VMEM((ROWS, t_width), bf16),
             pltpu.VMEM((8 * ROWS, width), bf16),
             pltpu.VMEM((8 * ROWS, t_width), bf16),
             pltpu.VMEM((16 * ROWS, width), bf16),
@@ -367,7 +422,7 @@
             pltpu.VMEM((7 * ROWS, width), bf16),
             pltpu.VMEM((7 * ROWS, width), bf16),
         ]
-        + [dma] * 18,
+        + [dma] * 19,
         compiler_params=pltpu.CompilerParams(
             collective_id=0, has_side_effects=True, vmem_limit_bytes=62 << 20
         ),

time: 96.5 us -> 86.3 us (0.89)
  Pallas kernels: 92.9 us -> 82.7 us
    pallas_call x1, Pallas kernels: 92.9 us -> 82.7 us  [body(): pl.pallas_call(kernel, out_shape=[jax.ShapeDtypeStruct((ROWS, width), f32...]
where the time goes in v4:
time: 86.3 us; the launch traced here: 86.1 us
  Pallas kernels  82.7 us (96%)
  local copies, waits for them, and re-layouts  2.8 us (3%)
    pallas_call x1, Pallas kernels, body(): pl.pallas_call(kernel, out_shape=[jax.ShapeDtypeStruct((ROWS, width), f32...  82.7 us
    unnamed x4, local copies, waits for them, and re-layouts  2.8 us

profile of v4, /device:TPU:0, one launch (start us, length us, event | category | flops | bytes accessed | tf_op | source)
XLA Modules:
  0.0 86.1 jit_solution(17355682428965062834)
XLA Ops:
  0.6 82.7 %shard_map.59 = (f32[128,1152]{1,0:T(8,128)}, f32[128,1152]{1,0:T(8,128)}) custom-call(bf16[128,1152]{1,0:T(8,128)(2,1)} %img_hbm.1, bf16[128,1152]{1,0:T(8,128)(2,1)} %txt_hbm.1, bf16[128,1536]{1,0:T(8,128)(2,1)} %timg_hbm.1, bf16[128,1536]{1,0:T(8,128)(2,1)} %ttxt_hbm.1), custom_call_target="tpu_custom_call" | custom-call | tf_op jit(solution)/shard_map/pallas_call | solution.py:397
  83.3 0.0 copy-start
  83.4 2.0 %copy.8 = f32[128,1152]{1,0:T(8,128)} copy(f32[128,1152]{1,0:T(8,128)} %get-tuple-element.4) | data formatting | bytes 1179648
  85.3 0.0 copy-done
  85.3 0.8 copy.9
Async XLA Ops:
  83.3 2.0 %copy-start = (f32[128,1152]{1,0:T(8,128)S(1)}, f32[128,1152]{1,0:T(8,128)}, u32[]{:S(2)}) copy-start(f32[128,1152]{1,0:T(8,128)} %get-tuple-element.5) | copy-start | bytes 1769476

commit v5 on v4

--- a/solution.py
+++ b/solution.py
@@ -37,8 +37,8 @@
 
 
 def kernel(
-    img_hbm, txt_hbm, timg_hbm, ttxt_hbm, image_grad, text_grad, img_raw, txt_raw, timg_raw, ttxt_raw,
-    si, ti, st, tt, pn2, pa2, pn3, pa3, gs, iacc, tacc, ib, tb, ts, crecv, irecv, trecv,
+    img_hbm, txt_hbm, timg_hbm, ttxt_hbm, grads, img_raw, txt_raw, timg_raw, ttxt_raw,
+    si, ti, st, tt, pa1, pn2, pa2, pn3, pa3, gs, iacc, tacc, ib, tb, ts, crecv, irecv, trecv,
     send_si, send_ti, send_st, send_tt, recv_si, recv_ti, recv_st, recv_tt,
     csend_st, csend_tt, crecv_st, crecv_tt, csend_g, crecv_g, load, isend, irsem, tsend, trsem,
 ):
@@ -183,7 +183,7 @@
         if diagonal:
             row = lax.broadcasted_iota(jnp.int32, (ROWS, WIDE), 0)
             col = lax.broadcasted_iota(jnp.int32, (ROWS, WIDE), 1)
-            positive = jnp.where(row == col + pair * WIDE, 1.0, 0.0)
+            positive = jnp.where(row == col, 1.0, 0.0)
             gs[0:ROWS] = (value[:ROWS] - positive).astype(jnp.bfloat16)
             gs[ROWS:count] = value[ROWS:].astype(jnp.bfloat16)
         else:
@@ -206,10 +206,10 @@
             hop(name, "3", "6", UP)
             hop(name, "3", "5", DOWN)
 
-    def near_across(names):
-        arrive(*[(name, part) for part in ("2b", "1a", "3") for name in names])
-        for slot in (1, 2, 3):
-            across(names[1], slot)
+    def near_across(name, chips):
+        for chip in chips:
+            arrive((name, {"3": "3", "1": "1a", "2": "2b"}[chip]))
+            across(name, slot_of[chip])
 
     def far_to_side(names):
         arrive(*[(name, part) for part in ("4a", "4b") for name in names])
@@ -225,17 +225,28 @@
     TEACHER, STUDENT = ("ti", "tt"), ("si", "st")
     relay(TEACHER)
     to_ring_first(STUDENT)
-    near_across(TEACHER)
+    near_across("tt", "312")
     far_to_side(TEACHER)
+    arrive(*[("ti", part) for part in ("3", "1a", "2b")])
+    arrive(*[("ttc", slot) for slot in range(4)])
+
+    def teach_first(pair):
+        pa1[pair] = teach(0, 512, pair)
+
+    over(0, 2, teach_first)
+    near_across("st", "3")
     relay(STUDENT)
+    arrive(("si", "3"))
     to_ring(TEACHER)
-    near_across(STUDENT)
     to_ring(STUDENT)
-
-    arrive(*[(name, slot) for slot in range(4) for name in ("ttc", "stc")])
-    learn(0, 512, 0, teach(0, 512, 0), True)
+    arrive(("stc", 0), ("stc", 1))
+    learn(0, 256, 0, pa1[0, 0:256], True)
+    near_across("st", "12")
+    arrive(("si", "1a"), ("si", "2b"))
+    learn(256, 256, 0, pa1[0, 256:512])
     far_to_side(STUDENT)
-    learn(0, 512, 1, teach(0, 512, 1))
+    arrive(("stc", 2), ("stc", 3))
+    learn(0, 512, 1, pa1[1])
 
     late_across("tt", "7")
     arrive(("ti", "7"))
@@ -352,26 +363,27 @@
         near = rows_of(in_buf[stream], "1").astype(jnp.float32) + rows_of(in_buf[stream], "2").astype(jnp.float32)
         return logit_scale * (part[stream]("0") + near + came(stream, "3"))
 
+    learn(768, 256, 1, pn3[1])
+    give((2, 3))
     learn(768, 256, 2, pn3[2])
     give((5, 4))
-    learn(768, 256, 1, pn3[1])
-    give((2, 3))
     arrive(("stc", 6), ("stc", 7))
-    learn(512, 256, 3, pa3[512:768])
-    arrive(("g", 5))
-    send_7("i")
-    send_7("t")
-    learn(0, 512, 3, pa3[0:512])
+    learn(256, 256, 3, pa3[256:512])
     send_near("i")
     arrive(("g", 2), ("g", 3))
     send_near("t")
+    learn(512, 256, 3, pa3[512:768])
+    send_7("i")
+    arrive(("g", 5))
+    send_7("t")
+    learn(0, 256, 3, pa3[0:256])
     learn(768, 256, 3, pa3[768:1024])
     give((6, 7))
     learn(768, 256, 0, pn3[0])
+    give((1, 0))
     send_56("i")
     arrive(("g", 6), ("g", 7))
     send_56("t")
-    give((1, 0))
     arrive(("g", 4))
     send_far("i")
     send_far("t")
@@ -380,9 +392,9 @@
     send_side("t")
     send_rest("i")
     send_rest("t")
-    image_grad[...] = back(total("i"), img_raw[...])
+    grads[0:ROWS] = back(total("i"), img_raw[...])
     arrive(("g", 0))
-    text_grad[...] = back(total("t"), txt_raw[...])
+    grads[ROWS : 2 * ROWS] = back(total("t"), txt_raw[...])
 
     for copy in sent:
         copy.wait_send()
@@ -394,11 +406,11 @@
     bf16, f32 = jnp.bfloat16, jnp.float32
     vmem = pl.BlockSpec(memory_space=pltpu.VMEM)
     dma = pltpu.SemaphoreType.DMA((10,))
-    return pl.pallas_call(
+    both = pl.pallas_call(
         kernel,
-        out_shape=[jax.ShapeDtypeStruct((ROWS, width), f32)] * 2,
+        out_shape=jax.ShapeDtypeStruct((2 * ROWS, width), f32),
         in_specs=[pl.BlockSpec(memory_space=pl.ANY)] * 4,
-        out_specs=[vmem] * 2,
+        out_specs=vmem,
         scratch_shapes=[
             pltpu.VMEM((ROWS, width), bf16),
             pltpu.VMEM((ROWS, width), bf16),
@@ -408,6 +420,7 @@
             pltpu.VMEM((8 * ROWS, t_width), bf16),
             pltpu.VMEM((16 * ROWS, width), bf16),
             pltpu.VMEM((16 * ROWS, t_width), bf16),
+            pltpu.VMEM((2, 4 * ROWS, 4 * ROWS), f32),
             pltpu.VMEM((2, 2 * ROWS, 4 * ROWS), f32),
             pltpu.VMEM((6 * ROWS, 4 * ROWS), f32),
             pltpu.VMEM((3, 2 * ROWS, 4 * ROWS), f32),
@@ -427,6 +440,7 @@
             collective_id=0, has_side_effects=True, vmem_limit_bytes=62 << 20
         ),
     )(student_img, student_txt, teacher_img, teacher_txt)
+    return both[:ROWS], both[ROWS:]
 
 
 def solution(mesh):

time: 86.3 us -> 82.8 us (0.959)
  Pallas kernels: 82.7 us -> 79.7 us
    pallas_call x1, Pallas kernels: 82.7 us -> 79.7 us  [body(): pl.pallas_call(kernel, out_shape=jax.ShapeDtypeStruct((2 * ROWS, width),...]
    unnamed x4 -> x0, local copies, waits for them, and re-layouts: 2.8 us -> none
    slice x0 -> x1, local copies, waits for them, and re-layouts: none -> 2.33 us  [body(): return (both[:ROWS], both[ROWS:])]
where the time goes in v5:
time: 82.8 us; the launch traced here: 82.6 us
  Pallas kernels  79.7 us (96%)
  local copies, waits for them, and re-layouts  2.33 us (3%)
    pallas_call x1, Pallas kernels, body(): pl.pallas_call(kernel, out_shape=jax.ShapeDtypeStruct((2 * ROWS, width),...  79.7 us
    slice x1, local copies, waits for them, and re-layouts, body(): return (both[:ROWS], both[ROWS:])  2.33 us

profile of v5, /device:TPU:0, one launch (start us, length us, event | category | flops | bytes accessed | tf_op | source)
XLA Modules:
  0.0 82.6 jit_solution(1931488292343840563)
XLA Ops:
  0.6 79.7 %shard_map.59 = f32[256,1152]{1,0:T(8,128)} custom-call(bf16[128,1152]{1,0:T(8,128)(2,1)} %img_hbm.1, bf16[128,1152]{1,0:T(8,128)(2,1)} %txt_hbm.1, bf16[128,1536]{1,0:T(8,128)(2,1)} %timg_hbm.1, bf16[128,1536]{1,0:T(8,128)(2,1)} %ttxt_hbm.1), custom_call_target="tpu_custom_call" | custom-call | tf_op jit(solution)/shard_map/pallas_call | solution.py:409
  80.3 2.3 %fusion = (f32[128,1152]{1,0:T(8,128)}, f32[128,1152]{1,0:T(8,128)}) fusion(f32[256,1152]{1,0:T(8,128)} %shard_map.59), kind=kLoop, calls=%fused_computation | loop fusion | bytes 2359296 | tf_op jit(solution)/shard_map/slice | solution.py:443

commit v6 on v5

--- a/solution.py
+++ b/solution.py
@@ -301,10 +301,13 @@
     peers = {"i": img_devs, "t": txt_devs}
     piece = {"1": (0, ROWS, 0), "2": (ROWS, ROWS, 1), "3": (2 * ROWS, ROWS, 2), "4": (3 * ROWS, ROWS, 3),
              "5": (4 * ROWS, ROWS, 4), "6": (5 * ROWS, ROWS, 5), "7": (6 * ROWS, ROWS, 6)}
-    for chip, first_sem in (("1", 0), ("2", 1), ("4", 3)):
-        row = piece[chip][0]
-        piece[chip + "a"] = (row, HALF, first_sem)
-        piece[chip + "b"] = (row + HALF, HALF, first_sem + 7 if chip != "4" else 9)
+    QUARTER = ROWS // 4
+    piece["1a"] = (0, HALF, 0)
+    piece["2b"] = (ROWS + HALF, HALF, 1)
+    for i, (chip, half) in enumerate((("1", "b"), ("2", "a"), ("4", "a"), ("4", "b"))):
+        row = piece[chip][0] + (HALF if half == "b" else 0)
+        for q in (0, 1):
+            piece[chip + half + str(q)] = (row + q * QUARTER, QUARTER, 7 + 2 * i + q)
 
     def rows_of(ref, key):
         row, count, _ = piece[key]
@@ -344,21 +347,24 @@
 
     def send_far(stream):
         fill(stream, "4", part[stream]("4") + came(stream, "7"))
-        put(stream, "4b", UP)
-        put(stream, "4a", DOWN)
+        for q in "01":
+            put(stream, "4b" + q, UP)
+            put(stream, "4a" + q, DOWN)
 
     def send_side(stream):
         fill(stream, "3", part[stream]("3") + came(stream, "5") + came(stream, "6"))
         put(stream, "3", SIDE)
 
-    def send_rest(stream):
-        fill(stream, "1b", part[stream]("1")[HALF:] + came(stream, "4b"))
-        fill(stream, "2a", part[stream]("2")[:HALF] + came(stream, "4a"))
-        put(stream, "1b", UP)
-        put(stream, "2a", DOWN)
+    def send_rest(stream, q):
+        low, high = q * QUARTER, (q + 1) * QUARTER
+        one, two, q = part[stream]("1"), part[stream]("2"), str(q)
+        fill(stream, "1b" + q, one[HALF + low : HALF + high] + came(stream, "4b" + q))
+        put(stream, "1b" + q, UP)
+        fill(stream, "2a" + q, two[low:high] + came(stream, "4a" + q))
+        put(stream, "2a" + q, DOWN)
 
     def total(stream):
-        for key in ("1a", "1b", "2a", "2b"):
+        for key in ("1a", "1b0", "1b1", "2a0", "2a1", "2b"):
             arrive((stream, "sum" + key))
         near = rows_of(in_buf[stream], "1").astype(jnp.float32) + rows_of(in_buf[stream], "2").astype(jnp.float32)
         return logit_scale * (part[stream]("0") + near + came(stream, "3"))
@@ -390,8 +396,9 @@
     arrive(("g", 1))
     send_side("i")
     send_side("t")
-    send_rest("i")
-    send_rest("t")
+    for q in (0, 1):
+        send_rest("i", q)
+        send_rest("t", q)
     grads[0:ROWS] = back(total("i"), img_raw[...])
     arrive(("g", 0))
     grads[ROWS : 2 * ROWS] = back(total("t"), txt_raw[...])
@@ -405,7 +412,7 @@
     t_width = teacher_img.shape[1]
     bf16, f32 = jnp.bfloat16, jnp.float32
     vmem = pl.BlockSpec(memory_space=pltpu.VMEM)
-    dma = pltpu.SemaphoreType.DMA((10,))
+    dma = pltpu.SemaphoreType.DMA((15,))
     both = pl.pallas_call(
         kernel,
         out_shape=jax.ShapeDtypeStruct((2 * ROWS, width), f32),

time: 82.8 us -> 83.5 us (level)
  no operation moved by 1% of the time
where the time goes in v6:
time: 83.5 us; the launch traced here: 83.4 us
  Pallas kernels  80.4 us (96%)
  local copies, waits for them, and re-layouts  2.33 us (3%)
    pallas_call x1, Pallas kernels, body(): pl.pallas_call(kernel, out_shape=jax.ShapeDtypeStruct((2 * ROWS, width),...  80.4 us
    slice x1, local copies, waits for them, and re-layouts, body(): return (both[:ROWS], both[ROWS:])  2.33 us

profile of v6, /device:TPU:0, one launch (start us, length us, event | category | flops | bytes accessed | tf_op | source)
XLA Modules:
  0.0 83.4 jit_solution(11192636310561989335)
XLA Ops:
  0.6 80.4 %shard_map.59 = f32[256,1152]{1,0:T(8,128)} custom-call(bf16[128,1152]{1,0:T(8,128)(2,1)} %img_hbm.1, bf16[128,1152]{1,0:T(8,128)(2,1)} %txt_hbm.1, bf16[128,1536]{1,0:T(8,128)(2,1)} %timg_hbm.1, bf16[128,1536]{1,0:T(8,128)(2,1)} %ttxt_hbm.1), custom_call_target="tpu_custom_call" | custom-call | tf_op jit(solution)/shard_map/pallas_call | solution.py:416
  81.0 2.3 %fusion = (f32[128,1152]{1,0:T(8,128)}, f32[128,1152]{1,0:T(8,128)}) fusion(f32[256,1152]{1,0:T(8,128)} %shard_map.59), kind=kLoop, calls=%fused_computation | loop fusion | bytes 2359296 | tf_op jit(solution)/shard_map/slice | solution.py:450

commit v7 on v6

--- a/solution.py
+++ b/solution.py
@@ -309,6 +309,11 @@
         for q in (0, 1):
             piece[chip + half + str(q)] = (row + q * QUARTER, QUARTER, 7 + 2 * i + q)
 
+    for chip, sems in (("3", (2, 3)), ("5", (4, 15)), ("6", (5, 16))):
+        row = piece[chip][0]
+        piece[chip + "a"] = (row, HALF, sems[0])
+        piece[chip + "b"] = (row + HALF, HALF, sems[1])
+
     def rows_of(ref, key):
         row, count, _ = piece[key]
         return ref[row : row + count]
@@ -342,8 +347,9 @@
     def send_56(stream):
         fill(stream, "5", part[stream]("5"))
         fill(stream, "6", part[stream]("6"))
-        put(stream, "5", UP)
-        put(stream, "6", DOWN)
+        for half in "ab":
+            put(stream, "5" + half, UP)
+            put(stream, "6" + half, DOWN)
 
     def send_far(stream):
         fill(stream, "4", part[stream]("4") + came(stream, "7"))
@@ -351,9 +357,11 @@
             put(stream, "4b" + q, UP)
             put(stream, "4a" + q, DOWN)
 
-    def send_side(stream):
-        fill(stream, "3", part[stream]("3") + came(stream, "5") + came(stream, "6"))
-        put(stream, "3", SIDE)
+    def send_side(stream, half):
+        low = 0 if half == "a" else HALF
+        own = part[stream]("3")[low : low + HALF]
+        fill(stream, "3" + half, own + came(stream, "5" + half) + came(stream, "6" + half))
+        put(stream, "3" + half, SIDE)
 
     def send_rest(stream, q):
         low, high = q * QUARTER, (q + 1) * QUARTER
@@ -364,10 +372,10 @@
         put(stream, "2a" + q, DOWN)
 
     def total(stream):
-        for key in ("1a", "1b0", "1b1", "2a0", "2a1", "2b"):
+        for key in ("1a", "1b0", "1b1", "2a0", "2a1", "2b", "3a", "3b"):
             arrive((stream, "sum" + key))
         near = rows_of(in_buf[stream], "1").astype(jnp.float32) + rows_of(in_buf[stream], "2").astype(jnp.float32)
-        return logit_scale * (part[stream]("0") + near + came(stream, "3"))
+        return logit_scale * (part[stream]("0") + near + rows_of(in_buf[stream], "3").astype(jnp.float32))
 
     learn(768, 256, 1, pn3[1])
     give((2, 3))
@@ -394,8 +402,9 @@
     send_far("i")
     send_far("t")
     arrive(("g", 1))
-    send_side("i")
-    send_side("t")
+    for half in "ab":
+        send_side("i", half)
+        send_side("t", half)
     for q in (0, 1):
         send_rest("i", q)
         send_rest("t", q)
@@ -412,7 +421,7 @@
     t_width = teacher_img.shape[1]
     bf16, f32 = jnp.bfloat16, jnp.float32
     vmem = pl.BlockSpec(memory_space=pltpu.VMEM)
-    dma = pltpu.SemaphoreType.DMA((15,))
+    dma = pltpu.SemaphoreType.DMA((17,))
     both = pl.pallas_call(
         kernel,
         out_shape=jax.ShapeDtypeStruct((2 * ROWS, width), f32),

time: 83.5 us -> 82.7 us (level)
  Pallas kernels: 80.4 us -> 79.3 us
    pallas_call x1, Pallas kernels: 80.4 us -> 79.3 us  [body(): pl.pallas_call(kernel, out_shape=jax.ShapeDtypeStruct((2 * ROWS, width),...]
where the time goes in v7:
time: 82.7 us; the launch traced here: 82.3 us
  Pallas kernels  79.3 us (96%)
  local copies, waits for them, and re-layouts  2.33 us (3%)
    pallas_call x1, Pallas kernels, body(): pl.pallas_call(kernel, out_shape=jax.ShapeDtypeStruct((2 * ROWS, width),...  79.3 us
    slice x1, local copies, waits for them, and re-layouts, body(): return (both[:ROWS], both[ROWS:])  2.33 us

profile of v7, /device:TPU:0, one launch (start us, length us, event | category | flops | bytes accessed | tf_op | source)
XLA Modules:
  0.0 82.3 jit_solution(17393621880428328229)
XLA Ops:
  0.6 79.3 %shard_map.59 = f32[256,1152]{1,0:T(8,128)} custom-call(bf16[128,1152]{1,0:T(8,128)(2,1)} %img_hbm.1, bf16[128,1152]{1,0:T(8,128)(2,1)} %txt_hbm.1, bf16[128,1536]{1,0:T(8,128)(2,1)} %timg_hbm.1, bf16[128,1536]{1,0:T(8,128)(2,1)} %ttxt_hbm.1), custom_call_target="tpu_custom_call" | custom-call | tf_op jit(solution)/shard_map/pallas_call | solution.py:425
  80.0 2.3 %fusion = (f32[128,1152]{1,0:T(8,128)}, f32[128,1152]{1,0:T(8,128)}) fusion(f32[256,1152]{1,0:T(8,128)} %shard_map.59), kind=kLoop, calls=%fused_computation | loop fusion | bytes 2359296 | tf_op jit(solution)/shard_map/slice | solution.py:459

commit v8 on v7

--- a/solution.py
+++ b/solution.py
@@ -261,10 +261,10 @@
     late_across("st", "7")
     arrive(("si", "7"))
     over(0, 2, lambda pair: learn(512, 256, pair, pn2[pair]))
+    late_across("tt", "56")
     arrive(("stc", 4), ("stc", 5))
     learn(0, 768, 2, pa2[...])
 
-    late_across("tt", "56")
     arrive(("ti", "5"), ("ti", "6"))
 
     def teach_new3(pair):
@@ -394,10 +394,10 @@
     learn(768, 256, 3, pa3[768:1024])
     give((6, 7))
     learn(768, 256, 0, pn3[0])
-    give((1, 0))
     send_56("i")
     arrive(("g", 6), ("g", 7))
     send_56("t")
+    give((1, 0))
     arrive(("g", 4))
     send_far("i")
     send_far("t")

time: 82.7 us -> 82.5 us (level)
  no operation moved by 1% of the time
where the time goes in v8:
time: 82.5 us; the launch traced here: 81.7 us
  Pallas kernels  78.7 us (95%)
  local copies, waits for them, and re-layouts  2.33 us (3%)
    pallas_call x1, Pallas kernels, body(): pl.pallas_call(kernel, out_shape=jax.ShapeDtypeStruct((2 * ROWS, width),...  78.7 us
    slice x1, local copies, waits for them, and re-layouts, body(): return (both[:ROWS], both[ROWS:])  2.33 us

profile of v8, /device:TPU:0, one launch (start us, length us, event | category | flops | bytes accessed | tf_op | source)
XLA Modules:
  0.0 81.7 jit_solution(10456385301264707806)
XLA Ops:
  0.6 78.7 %shard_map.59 = f32[256,1152]{1,0:T(8,128)} custom-call(bf16[128,1152]{1,0:T(8,128)(2,1)} %img_hbm.1, bf16[128,1152]{1,0:T(8,128)(2,1)} %txt_hbm.1, bf16[128,1536]{1,0:T(8,128)(2,1)} %timg_hbm.1, bf16[128,1536]{1,0:T(8,128)(2,1)} %ttxt_hbm.1), custom_call_target="tpu_custom_call" | custom-call | tf_op jit(solution)/shard_map/pallas_call | solution.py:425
  79.4 2.3 %fusion = (f32[128,1152]{1,0:T(8,128)}, f32[128,1152]{1,0:T(8,128)}) fusion(f32[256,1152]{1,0:T(8,128)} %shard_map.59), kind=kLoop, calls=%fused_computation | loop fusion | bytes 2359296 | tf_op jit(solution)/shard_map/slice | solution.py:459
